TPU v7x, 32 devices: a whole 2x2x4 slice. The times are simulated.
32 devices in a mesh: expert: 8 (over z, core), shard: 4 (over y, x).
Axes of the slice: x: 2, y: 2, z: 4, core: 2. Of those that a mesh axis runs over, the one named last changes fastest.
Arguments:
- hidden_in: bfloat16 [32, 256, 1024], P(('expert', 'shard')), may hold values from -6 to 6
- segment_ids: int32 [32, 256], P(('expert', 'shard')), may hold values from 0 to 3, never falling along the last dimension, each value on 1 to 128 neighbouring positions
- pad_mask: int32 [32, 256], P(('expert', 'shard')), may hold values from 0 to 1, as said below
- expert_choice: int32 [32, 256, 8], P(('expert', 'shard')), may hold values from 0 to 31, all different within a row
- slot_rank: int32 [32, 256], P(('expert', 'shard')), may hold values from 0 to 255, each once within a row
- attn_gain: bfloat16 [1024], P('shard'), may hold values from 0.5 to 1.5
- query_weight: bfloat16 [1024, 1024], P('shard'), may hold values from -0.1875 to 0.1875
- key_weight: bfloat16 [1024, 512], P('shard'), may hold values from -0.1875 to 0.1875
- value_weight: bfloat16 [1024, 512], P('shard'), may hold values from -0.1875 to 0.1875
- output_weight: bfloat16 [1024, 1024], P('shard'), may hold values from -1 to 1
- moe_gain: bfloat16 [1024], P('shard'), may hold values from 0.5 to 1.5
- router_weight: bfloat16 [1024, 32], P('shard'), may hold values from -0.25 to 0.25
- gate_weight: bfloat16 [32, 1024, 512], P('expert'), may hold values from -0.1875 to 0.1875
- up_weight: bfloat16 [32, 1024, 512], P('expert'), may hold values from -0.1875 to 0.1875
- down_weight: bfloat16 [32, 512, 1024], P('expert'), may hold values from -1 to 1
- out_grad: bfloat16 [32, 256, 1024], P(('expert', 'shard')), may hold values from -6 to 6
Outputs:
- block_out: bfloat16 [32, 256, 1024], P(('expert', 'shard'))
- in_grad: bfloat16 [32, 256, 1024], P(('expert', 'shard'))
- attn_gain_grad: float32 [1024], P('shard')
- query_weight_grad: float32 [1024, 1024], P('shard')
- key_weight_grad: float32 [1024, 512], P('shard')
- value_weight_grad: float32 [1024, 512], P('shard')
- output_weight_grad: float32 [1024, 1024], P('shard')
- moe_gain_grad: float32 [1024], P('shard')
- router_weight_grad: float32 [1024, 32], P('shard')
- gate_weight_grad: float32 [32, 1024, 512], P('expert')
- up_weight_grad: float32 [32, 1024, 512], P('expert')
- down_weight_grad: float32 [32, 512, 1024], P('expert')
Inputs may be any that keep to these rules, and one draw needn't show every extreme that they name: `segment_ids`: along each sequence the document numbers never fall; each document holds at most 128 tokens and one holds exactly that many. `pad_mask`: each sequence's live tokens (1) come first; its padded tail (0) holds at most 64 tokens, and some sequence has exactly that many. `expert_choice`: the 8 experts of a token are different. `slot_rank`: each sequence holds every number of 0 to 255 once.
All inputs are finite; a program needn't handle non-finite values.
Results may differ from a plain program's by a relative error of at most 0.02.
Values may be sent and summed in bfloat16 or wider, within the bound.
No kernel may reach another device: no remote copies, remote signals or barrier semaphores. Data moves between devices by JAX's collectives and lax.ppermute only.
A program may use at most 192 MiB of HBM per device.

v0:
```python
import jax
import jax.numpy as jnp
from jax import lax
from jax.sharding import PartitionSpec as P

HEADS = 16
KV_HEADS = 8
HEAD = 64


eps = 1e-05
masked = -1e30


def rope_tables(segments, head_size):
    length = segments.shape[0]
    positions = jnp.arange(length, dtype=jnp.int32)
    starts = jnp.concatenate([jnp.ones((1,), dtype=bool), segments[1:] != segments[:-1]])
    doc_start = lax.cummax(jnp.where(starts, positions, 0), axis=0)
    places = (positions - doc_start).astype(jnp.float32)
    half_size = head_size // 2
    frequency = 10000.0 ** (-jnp.arange(half_size, dtype=jnp.float32) * 2.0 / head_size)
    angles = places[:, None] * frequency[None, :]
    cosine = jnp.concatenate([jnp.cos(angles), jnp.cos(angles)], -1)
    sine_table = jnp.concatenate([jnp.sin(angles), jnp.sin(angles)], -1)
    return (cosine, sine_table)


def rotate(values, cosine, sine_table):
    half_size = values.shape[-1] // 2
    turned = jnp.concatenate([-values[..., half_size:], values[..., :half_size]], -1)
    return values * cosine[:, None, :] + turned * sine_table[:, None, :]


def unrotate(grads, cosine, sine_table):
    half_size = grads.shape[-1] // 2
    scaled = grads * sine_table[:, None, :]
    turned = jnp.concatenate([scaled[..., half_size:], -scaled[..., :half_size]], -1)
    return grads * cosine[:, None, :] + turned


def allowed_mask(segments, live_int):
    length = segments.shape[0]
    rows_idx = jnp.arange(length, dtype=jnp.int32)[:, None]
    cols_idx = jnp.arange(length, dtype=jnp.int32)[None, :]
    same_doc = segments[:, None] == segments[None, :]
    return same_doc & (cols_idx <= rows_idx) & (live_int[None, :] > 0) | (cols_idx == rows_idx)


def norm_back(grad_in, normed, factor):
    return factor * (grad_in - normed * jnp.mean(grad_in * normed, -1, keepdims=True))


def per_device(
    hidden_in,
    segment_ids,
    pad_mask,
    expert_choice,
    slot_rank,
    attn_gain,
    query_weight,
    key_weight,
    value_weight,
    output_weight,
    moe_gain,
    router_weight,
    gate_weight,
    up_weight,
    down_weight,
    out_grad,
):
    gathered = (
        lax.all_gather(attn_gain, "shard", axis=0, tiled=True),
        lax.all_gather(query_weight, "shard", axis=0, tiled=True),
        lax.all_gather(key_weight, "shard", axis=0, tiled=True),
        lax.all_gather(value_weight, "shard", axis=0, tiled=True),
        lax.all_gather(output_weight, "shard", axis=0, tiled=True),
        lax.all_gather(moe_gain, "shard", axis=0, tiled=True),
        lax.all_gather(router_weight, "shard", axis=0, tiled=True),
    )
    gain_one, query_full, key_full, value_full, output_full, gain_two, router_full = gathered
    gain_one = gain_one.astype(jnp.float32)
    gain_two = gain_two.astype(jnp.float32)
    hidden = hidden_in[0].astype(jnp.float32)
    length, width = hidden.shape
    segments = segment_ids[0]
    live_int = pad_mask[0]
    live = live_int.astype(jnp.float32)
    choices = expert_choice[0]
    ranks = slot_rank[0]
    top_count = choices.shape[1]
    local_experts = gate_weight.shape[0]
    owners = lax.axis_size("expert")
    experts_all = owners * local_experts
    capacity = length * top_count // experts_all
    slot_total = experts_all * capacity
    kv_groups = HEADS // KV_HEADS
    score_scale = HEAD ** (-0.5)
    inv_one = lax.rsqrt(jnp.mean(hidden * hidden, -1, keepdims=True) + eps)
    normed_one = hidden * inv_one
    attn_in = (normed_one * gain_one).astype(jnp.bfloat16)
    cosine, sine_table = rope_tables(segments, HEAD)
    query_raw = jnp.dot(attn_in, query_full, preferred_element_type=jnp.float32).reshape(
        length, HEADS, HEAD
    )
    query_rot = (
        rotate(query_raw, cosine, sine_table)
        .astype(jnp.bfloat16)
        .reshape(length, KV_HEADS, kv_groups, HEAD)
    )
    key_raw = jnp.dot(attn_in, key_full, preferred_element_type=jnp.float32).reshape(
        length, KV_HEADS, HEAD
    )
    key_rot = rotate(key_raw, cosine, sine_table).astype(jnp.bfloat16)
    value_rows = (
        jnp.dot(attn_in, value_full, preferred_element_type=jnp.float32)
        .astype(jnp.bfloat16)
        .reshape(length, KV_HEADS, HEAD)
    )
    allowed = allowed_mask(segments, live_int)

    def score_block():
        raw_scores = (
            jnp.einsum("qgrd,kgd->grqk", query_rot, key_rot, preferred_element_type=jnp.float32)
            * score_scale
        )
        return jnp.where(allowed[None, None], raw_scores, masked)

    scores = score_block()
    top_score = jnp.max(scores, -1, keepdims=True)
    log_total = top_score + jnp.log(jnp.sum(jnp.exp(scores - top_score), -1, keepdims=True))
    probs = jnp.exp(scores - log_total)
    mixed = jnp.einsum(
        "grqk,kgd->qgrd", probs.astype(jnp.bfloat16), value_rows, preferred_element_type=jnp.float32
    )
    attn_out = mixed.astype(jnp.bfloat16).reshape(length, HEADS * HEAD)
    resid_one = hidden + jnp.dot(attn_out, output_full, preferred_element_type=jnp.float32)
    inv_two = lax.rsqrt(jnp.mean(resid_one * resid_one, -1, keepdims=True) + eps)
    normed_two = resid_one * inv_two
    moe_in = (normed_two * gain_two).astype(jnp.bfloat16)
    logits = jnp.dot(moe_in, router_full, preferred_element_type=jnp.float32)
    picked = choices[:, :, None] == jnp.arange(experts_all, dtype=jnp.int32)[None, None, :]
    chosen = jnp.sum(jnp.where(picked, logits[:, None, :], 0.0), -1)
    chosen_exp = jnp.exp(chosen - jnp.max(chosen, -1, keepdims=True))
    gates = chosen_exp / jnp.sum(chosen_exp, -1, keepdims=True)
    active = jnp.sum(picked.astype(jnp.int32), 1) * live_int[:, None]
    by_rank = jnp.zeros_like(active).at[ranks].set(active)
    earlier = jnp.cumsum(by_rank, 0) - by_rank
    place_all = earlier[ranks]
    places = jnp.sum(jnp.where(picked, place_all[:, None, :], 0), -1)
    kept = (live_int[:, None] > 0) & (places < capacity)
    pair_weights = jnp.where(kept, gates, 0.0)
    flat_pairs = jnp.where(kept, choices * capacity + places, slot_total)
    flat_list = flat_pairs.reshape(-1)
    token_list = jnp.broadcast_to(
        jnp.arange(length, dtype=jnp.int32)[:, None], (length, top_count)
    ).reshape(-1)
    slot_token = (
        jnp.full((slot_total + 1,), length, jnp.int32).at[flat_list].set(token_list)[:slot_total]
    )
    slot_weight = (
        jnp.zeros((slot_total + 1,), jnp.float32)
        .at[flat_list]
        .set(pair_weights.reshape(-1))[:slot_total]
    )
    moe_padded = jnp.concatenate([moe_in, jnp.zeros((1, width), jnp.bfloat16)], 0)
    send_rows = moe_padded[slot_token].reshape(owners, local_experts, capacity, width)
    rows_in = lax.all_to_all(send_rows, "expert", split_axis=0, concat_axis=0, tiled=True)
    expert_gate_pre = jnp.einsum(
        "sjcd,jdf->sjcf", rows_in, gate_weight, preferred_element_type=jnp.float32
    )
    expert_up_pre = jnp.einsum(
        "sjcd,jdf->sjcf", rows_in, up_weight, preferred_element_type=jnp.float32
    )
    expert_act_rows = (expert_gate_pre * jax.nn.sigmoid(expert_gate_pre) * expert_up_pre).astype(
        jnp.bfloat16
    )
    outs_rows = jnp.einsum(
        "sjcf,jfd->sjcd", expert_act_rows, down_weight, preferred_element_type=jnp.float32
    ).astype(jnp.bfloat16)
    results = (outs_rows, rows_in, expert_gate_pre, expert_up_pre)
    rows_home = results[1]
    back_rows = lax.all_to_all(
        results[0], "expert", split_axis=0, concat_axis=0, tiled=True
    ).reshape(slot_total, width)
    back_padded = jnp.concatenate([back_rows, jnp.zeros((1, width), jnp.bfloat16)], 0)
    from_experts = back_padded[flat_pairs].astype(jnp.float32)
    moe_branch = jnp.sum(pair_weights[:, :, None] * from_experts, 1)
    resid_two = resid_one + moe_branch
    block_out = (live[:, None] * resid_two).astype(jnp.bfloat16)
    grad_two = live[:, None] * out_grad[0].astype(jnp.float32)
    gate_grads = jnp.where(kept, jnp.sum(grad_two[:, None, :] * from_experts, -1), 0.0)
    grad_padded = jnp.concatenate([grad_two, jnp.zeros((1, width), jnp.float32)], 0)
    slot_grads = (
        (slot_weight[:, None] * grad_padded[slot_token])
        .astype(jnp.bfloat16)
        .reshape(owners, local_experts, capacity, width)
    )
    owner_grads = lax.all_to_all(slot_grads, "expert", split_axis=0, concat_axis=0, tiled=True)
    row_grads = []
    gate_terms = []
    up_terms = []
    down_terms = []
    for expert_idx in range(local_experts):
        rows_one = rows_home[:, expert_idx]
        gate_pre = results[2][:, expert_idx]
        up_pre = results[3][:, expert_idx]
        sigma = jax.nn.sigmoid(gate_pre)
        silu_vals = gate_pre * sigma
        act_rows = (silu_vals * up_pre).astype(jnp.bfloat16)
        grad_out = owner_grads[:, expert_idx]
        act_grads = jnp.einsum(
            "scd,fd->scf", grad_out, down_weight[expert_idx], preferred_element_type=jnp.float32
        )
        gate_pre_grads = (act_grads * up_pre * sigma * (1.0 + gate_pre * (1.0 - sigma))).astype(
            jnp.bfloat16
        )
        up_pre_grads = (act_grads * silu_vals).astype(jnp.bfloat16)
        rows_grad = jnp.einsum(
            "scf,df->scd",
            gate_pre_grads,
            gate_weight[expert_idx],
            preferred_element_type=jnp.float32,
        )
        rows_grad = rows_grad + jnp.einsum(
            "scf,df->scd", up_pre_grads, up_weight[expert_idx], preferred_element_type=jnp.float32
        )
        row_grads.append(rows_grad.astype(jnp.bfloat16))
        expert_terms = (
            jnp.einsum("scd,scf->df", rows_one, gate_pre_grads, preferred_element_type=jnp.float32),
            jnp.einsum("scd,scf->df", rows_one, up_pre_grads, preferred_element_type=jnp.float32),
            jnp.einsum("scf,scd->fd", act_rows, grad_out, preferred_element_type=jnp.float32),
        )
        gate_terms.append(expert_terms[0])
        up_terms.append(expert_terms[1])
        down_terms.append(expert_terms[2])
    expert_sums = (jnp.stack(gate_terms), jnp.stack(up_terms), jnp.stack(down_terms))
    expert_sums = (
        lax.psum(expert_sums[0].astype(jnp.bfloat16), "shard").astype(jnp.float32),
        lax.psum(expert_sums[1].astype(jnp.bfloat16), "shard").astype(jnp.float32),
        lax.psum(expert_sums[2].astype(jnp.bfloat16), "shard").astype(jnp.float32),
    )
    grads_home = jnp.stack(row_grads, 1)
    grads_back = lax.all_to_all(
        grads_home, "expert", split_axis=0, concat_axis=0, tiled=True
    ).reshape(slot_total, width)
    grads_padded = jnp.concatenate([grads_back, jnp.zeros((1, width), jnp.bfloat16)], 0)
    expert_part = jnp.sum(grads_padded[flat_pairs].astype(jnp.float32), 1)
    gate_inner = jnp.sum(gates * gate_grads, -1, keepdims=True)
    chosen_grads = gates * (gate_grads - gate_inner)
    logit_grads = jnp.sum(jnp.where(picked, chosen_grads[:, :, None], 0.0), 1).astype(jnp.bfloat16)
    router_grad = jnp.einsum("ld,le->de", moe_in, logit_grads, preferred_element_type=jnp.float32)
    moe_in_grads = expert_part + jnp.einsum(
        "le,de->ld", logit_grads, router_full, preferred_element_type=jnp.float32
    )
    gain_two_grad = jnp.sum(moe_in_grads * normed_two, 0)
    resid_grad = grad_two + norm_back(moe_in_grads * gain_two, normed_two, inv_two)
    branch_grad = resid_grad.astype(jnp.bfloat16)
    output_grad_w = jnp.einsum(
        "lh,ld->hd", attn_out, branch_grad, preferred_element_type=jnp.float32
    )
    mixed_grad = jnp.einsum(
        "ld,hd->lh", branch_grad, output_full, preferred_element_type=jnp.float32
    )
    mixed_grad = mixed_grad.astype(jnp.bfloat16).reshape(length, KV_HEADS, kv_groups, HEAD)
    probs_again = jnp.exp(score_block() - log_total)
    prob_grads = jnp.einsum(
        "qgrd,kgd->grqk", mixed_grad, value_rows, preferred_element_type=jnp.float32
    )
    value_grad = jnp.einsum(
        "grqk,qgrd->kgd",
        probs_again.astype(jnp.bfloat16),
        mixed_grad,
        preferred_element_type=jnp.float32,
    )
    value_grad = value_grad.astype(jnp.bfloat16).reshape(length, KV_HEADS * HEAD)
    score_grads = (
        probs_again * (prob_grads - jnp.sum(probs_again * prob_grads, -1, keepdims=True))
    ).astype(jnp.bfloat16)
    query_rot_grad = (
        jnp.einsum("grqk,kgd->qgrd", score_grads, key_rot, preferred_element_type=jnp.float32)
        * score_scale
    )
    key_rot_grad = (
        jnp.einsum("grqk,qgrd->kgd", score_grads, query_rot, preferred_element_type=jnp.float32)
        * score_scale
    )
    query_grad = (
        unrotate(query_rot_grad.reshape(length, HEADS, HEAD), cosine, sine_table)
        .astype(jnp.bfloat16)
        .reshape(length, HEADS * HEAD)
    )
    key_grad = (
        unrotate(key_rot_grad, cosine, sine_table)
        .astype(jnp.bfloat16)
        .reshape(length, KV_HEADS * HEAD)
    )
    query_grad_w = jnp.einsum("ld,lh->dh", attn_in, query_grad, preferred_element_type=jnp.float32)
    key_grad_w = jnp.einsum("ld,lh->dh", attn_in, key_grad, preferred_element_type=jnp.float32)
    value_grad_w = jnp.einsum("ld,lh->dh", attn_in, value_grad, preferred_element_type=jnp.float32)
    attn_in_grads = jnp.einsum(
        "lh,dh->ld", query_grad, query_full, preferred_element_type=jnp.float32
    )
    attn_in_grads = attn_in_grads + jnp.einsum(
        "lh,dh->ld", key_grad, key_full, preferred_element_type=jnp.float32
    )
    attn_in_grads = attn_in_grads + jnp.einsum(
        "lh,dh->ld", value_grad, value_full, preferred_element_type=jnp.float32
    )
    gain_one_grad = jnp.sum(attn_in_grads * normed_one, 0)
    hidden_grad = resid_grad + norm_back(attn_in_grads * gain_one, normed_one, inv_one)
    mixer_terms = (
        gain_one_grad,
        query_grad_w,
        key_grad_w,
        value_grad_w,
        output_grad_w,
        gain_two_grad,
        router_grad,
    )
    mixer_part = (
        lax.psum_scatter(
            mixer_terms[0].astype(jnp.bfloat16), "shard", scatter_dimension=0, tiled=True
        ).astype(jnp.float32),
        lax.psum_scatter(
            mixer_terms[1].astype(jnp.bfloat16), "shard", scatter_dimension=0, tiled=True
        ).astype(jnp.float32),
        lax.psum_scatter(
            mixer_terms[2].astype(jnp.bfloat16), "shard", scatter_dimension=0, tiled=True
        ).astype(jnp.float32),
        lax.psum_scatter(
            mixer_terms[3].astype(jnp.bfloat16), "shard", scatter_dimension=0, tiled=True
        ).astype(jnp.float32),
        lax.psum_scatter(
            mixer_terms[4].astype(jnp.bfloat16), "shard", scatter_dimension=0, tiled=True
        ).astype(jnp.float32),
        lax.psum_scatter(
            mixer_terms[5].astype(jnp.bfloat16), "shard", scatter_dimension=0, tiled=True
        ).astype(jnp.float32),
        lax.psum_scatter(
            mixer_terms[6].astype(jnp.bfloat16), "shard", scatter_dimension=0, tiled=True
        ).astype(jnp.float32),
    )
    mixer_sum = (
        lax.psum(mixer_part[0].astype(jnp.bfloat16), "expert").astype(jnp.float32),
        lax.psum(mixer_part[1].astype(jnp.bfloat16), "expert").astype(jnp.float32),
        lax.psum(mixer_part[2].astype(jnp.bfloat16), "expert").astype(jnp.float32),
        lax.psum(mixer_part[3].astype(jnp.bfloat16), "expert").astype(jnp.float32),
        lax.psum(mixer_part[4].astype(jnp.bfloat16), "expert").astype(jnp.float32),
        lax.psum(mixer_part[5].astype(jnp.bfloat16), "expert").astype(jnp.float32),
        lax.psum(mixer_part[6].astype(jnp.bfloat16), "expert").astype(jnp.float32),
    )
    return (
        block_out[None],
        hidden_grad.astype(jnp.bfloat16)[None],
        mixer_sum[0],
        mixer_sum[1],
        mixer_sum[2],
        mixer_sum[3],
        mixer_sum[4],
        mixer_sum[5],
        mixer_sum[6],
        expert_sums[0],
        expert_sums[1],
        expert_sums[2],
    )


def solution(mesh):
    in_specs = (
        P(("expert", "shard"), None, None),
        P(("expert", "shard"), None),
        P(("expert", "shard"), None),
        P(("expert", "shard"), None, None),
        P(("expert", "shard"), None),
        P("shard"),
        P("shard", None),
        P("shard", None),
        P("shard", None),
        P("shard", None),
        P("shard"),
        P("shard", None),
        P("expert", None, None),
        P("expert", None, None),
        P("expert", None, None),
        P(("expert", "shard"), None, None),
    )
    out_specs = (
        P(("expert", "shard"), None, None),
        P(("expert", "shard"), None, None),
        P("shard"),
        P("shard", None),
        P("shard", None),
        P("shard", None),
        P("shard", None),
        P("shard"),
        P("shard", None),
        P("expert", None, None),
        P("expert", None, None),
        P("expert", None, None),
    )
    return jax.shard_map(
        per_device, mesh=mesh, in_specs=in_specs, out_specs=out_specs, check_vma=False
    )
```

profile of v0, /device:TPU:0, one launch (start us, length us, event | category | flops | bytes accessed | tf_op | source)
XLA Modules:
  0.0 1073.5 jit_solution(8076174625313281137)
XLA Ops:
  16.2 9.6 all-gather.1
  25.8 8.1 all-gather
  41.0 8.1 scatter_custom_fusion.1
  51.7 15.8 %all-gather.9.cloned.1.call-done = bf16[1024,512]{1,0:T(8,128)(2,1)} async-done(((bf16[256,512]{1,0:T(8,128)(2,1)}), bf16[1024,512]{1,0:T(8,128)(2,1)}) %all-gather.9.cloned.1.call-update) | async-done | bytes 1048592 | tf_op jit(solution)/shard_map/all_gather | solution.py:75
  67.5 2.3 copy.158
  71.7 32.9 %all-gather.11.cloned.1.call-done = bf16[1024,1024]{1,0:T(8,128)(2,1)} async-done(((bf16[256,1024]{1,0:T(8,128)(2,1)}), bf16[1024,1024]{1,0:T(8,128)(2,1)}) %all-gather.11.cloned.1.call-update) | async-done | bytes 2097168 | tf_op jit(solution)/shard_map/all_gather | solution.py:74
  104.6 3.9 copy.159
  108.5 2.4 fusion.103
  115.9 25.6 %all-gather.13.cloned.1.call-done = bf16[1024,1024]{1,0:T(8,128)(2,1)} async-done(((bf16[256,1024]{1,0:T(8,128)(2,1)}), bf16[1024,1024]{1,0:T(8,128)(2,1)}) %all-gather.13.cloned.1.call-update) | async-done | bytes 2097168 | tf_op jit(solution)/shard_map/all_gather | solution.py:77
  141.5 2.4 multiply_reduce_fusion.2
  144.7 9.6 gather_fusion.1
  154.3 4.7 all-to-all-start
  160.8 9.7 gather_fusion.3
  170.5 8.6 all_gather.27
  181.5 8.2 scatter_custom_fusion.2
  189.8 5.8 multiply_convert_fusion
  195.7 57.4 %all-to-all-done = bf16[8,4,64,1024]{3,2,1,0:T(8,128)(2,1)} async-done(((bf16[8,4,64,1024]{3,2,1,0:T(8,128)(2,1)}), bf16[8,4,64,1024]{3,2,1,0:T(8,128)(2,1)}, u32[]{:S(2)}, u32[]{:S(2)}) %all-to-all-start) | async-done | bytes 4194336 | tf_op jit(solution)/shard_map/all_to_all | solution.py:168
  253.1 4.6 all-to-all-start.2
  257.7 5.9 fusion.15
  263.7 6.1 fusion.18
  269.8 2.4 convert_bitcast_fusion
  272.2 2.5 copy.172
  274.7 77.0 %all-to-all-done.2 = bf16[8,4,64,1024]{3,2,1,0:T(8,128)(2,1)} async-done(((bf16[8,4,64,1024]{3,2,1,0:T(8,128)(2,1)}), bf16[8,4,64,1024]{3,2,1,0:T(8,128)(2,1)}, u32[]{:S(2)}, u32[]{:S(2)}) %all-to-all-start.2) | async-done | bytes 4194336 | tf_op jit(solution)/shard_map/all_to_all | solution.py:199
  351.7 5.0 all-to-all-start.1
  356.7 2.4 fusion.69
  359.1 2.3 fusion.74
  363.5 5.5 multiply_convert_fusion.14
  375.7 2.5 copy.179
  378.2 72.5 %all-to-all-done.1 = bf16[8,4,64,1024]{3,2,1,0:T(8,128)(2,1)} async-done(((bf16[8,4,64,1024]{3,2,1,0:T(8,128)(2,1)}), bf16[8,4,64,1024]{3,2,1,0:T(8,128)(2,1)}, u32[]{:S(2)}, u32[]{:S(2)}) %all-to-all-start.1) | async-done | bytes 4194336 | tf_op jit(solution)/shard_map/all_to_all | solution.py:183
  450.7 4.6 all-to-all-start.3
  455.6 4.6 concatenate.44
  460.2 14.0 %gather_fusion.2 = bf16[2048,1024]{1,0:T(8,128)(2,1)} fusion(bf16[2049,1024]{1,0:T(8,128)(2,1)} %concatenate.44, s32[2048]{0:T(1024)S(1)} %broadcast_clamp_fusion), kind=kCustom, calls=%fused_computation.2 | custom fusion | bytes 8396800 | tf_op jit(solution)/shard_map/gather | solution.py:187
  474.2 6.1 fusion.1
  481.4 67.8 %all-to-all-done.3 = bf16[8,4,64,1024]{3,2,1,0:T(8,128)(2,1)} async-done(((bf16[8,4,64,1024]{3,2,1,0:T(8,128)(2,1)}), bf16[8,4,64,1024]{3,2,1,0:T(8,128)(2,1)}, u32[]{:S(2)}, u32[]{:S(2)}) %all-to-all-start.3) | async-done | bytes 4194336 | tf_op jit(solution)/shard_map/all_to_all | solution.py:244
  549.2 4.6 concatenate.46
  553.9 13.7 %gather_fusion.4 = bf16[2048,1024]{1,0:T(8,128)(2,1)} fusion(bf16[2049,1024]{1,0:T(8,128)(2,1)} %concatenate.46, s32[2048]{0:T(1024)S(1)} %broadcast_clamp_fusion), kind=kCustom, calls=%fused_computation.4 | custom fusion | bytes 8396800 | tf_op jit(solution)/shard_map/gather | solution.py:248
  567.6 5.6 convert_reduce_fusion
  576.1 3.3 fusion.44
  581.3 3.7 fusion.8
  596.7 2.2 convolution_convert_fusion.1
  599.0 3.2 fusion.22
  602.1 3.0 fusion.25
  605.1 3.0 fusion.24
  608.2 3.0 fusion.23
  611.2 3.1 fusion.28
  614.3 3.1 fusion.27
  625.6 2.3 pad_maximum_fusion.3
  628.9 3.1 fusion.29
  632.0 6.3 reduce-scatter.8.cloned.1.call-done
  638.3 38.2 %reduce-scatter.12.cloned.1.call-done = bf16[256,1024]{1,0:T(8,128)(2,1)} async-done(((bf16[1024,1024]{1,0:T(8,128)(2,1)}), bf16[256,1024]{1,0:T(8,128)(2,1)}) %reduce-scatter.12.cloned.1.call-update) | async-done | bytes 524304 | tf_op jit(solution)/shard_map/reduce_scatter | solution.py:334
  676.5 38.8 %reduce-scatter.6.cloned.1.call-done = bf16[256,1024]{1,0:T(8,128)(2,1)} async-done(((bf16[1024,1024]{1,0:T(8,128)(2,1)}), bf16[256,1024]{1,0:T(8,128)(2,1)}) %reduce-scatter.6.cloned.1.call-update) | async-done | bytes 524304 | tf_op jit(solution)/shard_map/reduce_scatter | solution.py:325
  715.4 2.1 fusion.26
  717.8 2.4 pad_maximum_fusion.1
  721.2 2.3 pad_maximum_fusion.2
  726.9 2.4 fusion.158
  730.6 8.9 all-reduce.8
  742.6 29.0 %all-reduce.6 = (bf16[256]{0:T(256)(128)(2,1)S(1)}, bf16[256]{0:T(256)(128)(2,1)S(1)}, bf16[256,32]{0,1:T(8,128)(2,1)S(1)}) all-reduce(bf16[256]{0:T(256)(128)(2,1)S(1)} %dynamic-slice.1, bf16[256]{0:T(256)(128)(2,1)S(1)} %dynamic-slice.3, ...), channel_id=1, replica_groups=mesh['expert'=8,'shard'=4] {'expert'}, use_global_device_ids=true, to_apply=%region_26.27 | all-reduce | flops 8704 | bytes 34816 | tf_op jit(solution)/shard_map/psum | solution.py:345
  773.4 34.2 %all-reduce.13.cloned.1.call-done = (bf16[256,1024]{1,0:T(8,128)(2,1)}, bf16[256,512]{1,0:T(8,128)(2,1)}, bf16[256,512]{1,0:T(8,128)(2,1)}, bf16[256,1024]{1,0:T(8,128)(2,1)}) async-done(((bf16[256,1024]{1,0:T(8,128)(2,1)}, bf16[256,512]{1,0:T(8,128)(2,1)}, bf16[256,512]{1,0:T(8,128)(2,1)}, bf16[256,1024]{1,0:T(8,128)(2,1)}), (bf16[256,1024]{1,0:T(8,128)(2,1)}, bf16[256,512]{1,0:T(8,128)(2,1)}, ...) | async-done | bytes 1572880 | tf_op jit(solution)/shard_map/psum | solution.py:346
  807.6 2.1 convert_element_type.310
  813.3 2.1 convert_element_type.316
  815.4 235.2 %all-reduce.15.cloned.1.call-done = (bf16[4,1024,512]{2,1,0:T(8,128)(2,1)}, bf16[4,1024,512]{2,1,0:T(8,128)(2,1)}, bf16[4,512,1024]{2,1,0:T(8,128)(2,1)}) async-done(((bf16[4,1024,512]{2,1,0:T(8,128)(2,1)}, bf16[4,1024,512]{2,1,0:T(8,128)(2,1)}, bf16[4,512,1024]{2,1,0:T(8,128)(2,1)}), (bf16[4,1024,512]{2,1,0:T(8,128)(2,1)}, bf16[4,1024,512]{2,1,0:T(8,128)(2,1)}, ...) | async-done | bytes 12582928 | tf_op jit(solution)/shard_map/psum | solution.py:239
  1050.6 6.9 convert_element_type.321
  1057.6 4.6 convert_element_type.322
  1062.1 4.4 convert_element_type.327
  (311 shorter events, 79.4 us)
Async XLA Ops:
  7.2 42.5 %copy-start.64 = (s32[1,256]{1,0:T(1,128)S(1)}, s32[1,256]{1,0:T(1,128)}, u32[]{:S(2)}) copy-start(s32[1,256]{1,0:T(1,128)} %param.17) | copy-start | bytes 3076
  7.2 42.7 %copy-start.2 = (bf16[1,256,1024]{2,1,0:T(8,128)(2,1)S(1)}, bf16[1,256,1024]{2,1,0:T(8,128)(2,1)}, u32[]{:S(2)}) copy-start(bf16[1,256,1024]{2,1,0:T(8,128)(2,1)} %param.16) | copy-start | bytes 1572868
  7.2 32.2 %copy-start.54 = (s32[1,256,8]{1,2,0:T(8,128)S(1)}, s32[1,256,8]{1,2,0:T(8,128)}, u32[]{:S(2)}) copy-start(s32[1,256,8]{1,2,0:T(8,128)} %param.19) | copy-start | bytes 24580
  7.2 42.6 %all-gather.7.cloned.1.call-start = ((), (), s32[]{:S(2)}) async-start(), calls=%async_computation.9 | async-start | bytes 1310720 | tf_op jit(solution)/shard_map/all_gather | solution.py:76
  7.9 59.6 %all-gather.9.cloned.1.call-start = ((), (), s32[]{:S(2)}) async-start(), calls=%async_computation.10 | async-start | bytes 1310720 | tf_op jit(solution)/shard_map/all_gather | solution.py:75
  8.7 95.9 %all-gather.11.cloned.1.call-start = ((), (), s32[]{:S(2)}) async-start(), calls=%async_computation.11 | async-start | bytes 2621440 | tf_op jit(solution)/shard_map/all_gather | solution.py:74
  9.4 132.0 %all-gather.13.cloned.1.call-start = ((), (), s32[]{:S(2)}) async-start(), calls=%async_computation.12 | async-start | bytes 2621440 | tf_op jit(solution)/shard_map/all_gather | solution.py:77
  11.4 23.1 %copy-start.70 = (pred[256]{0:T(512)(128)(4,1)}, pred[256]{0:T(512)(128)(4,1)S(1)}, u32[]{:S(2)}) copy-start(pred[256]{0:T(512)(128)(4,1)S(1)} %broadcast_compare_fusion) | copy-start | bytes 772
  16.2 92.3 %copy-start.57 = (f32[256]{0:T(256)}, f32[256]{0:T(256)S(1)}, u32[]{:S(2)}) copy-start(f32[256]{0:T(256)S(1)} %add_rsqrt_fusion.1) | copy-start | bytes 3076
  40.3 70.7 %copy-start.22 = (f32[256,64]{0,1:T(8,128)}, f32[256,64]{0,1:T(8,128)S(1)}, u32[]{:S(2)}) copy-start(f32[256,64]{0,1:T(8,128)S(1)} %get-tuple-element.53) | copy-start | bytes 196612
  40.9 8.1 copy-start.69
  49.7 61.3 %copy-start.25 = (f32[256,64]{0,1:T(8,128)}, f32[256,64]{0,1:T(8,128)S(1)}, u32[]{:S(2)}) copy-start(f32[256,64]{0,1:T(8,128)S(1)} %get-tuple-element.55) | copy-start | bytes 196612
  51.7 62.0 %copy-start.26 = (bf16[256,512]{0,1:T(8,128)(2,1)}, bf16[256,512]{0,1:T(8,128)(2,1)S(1)}, u32[]{:S(2)}) copy-start(bf16[256,512]{0,1:T(8,128)(2,1)S(1)} %copy.157) | copy-start | bytes 786436
  115.9 28.0 %copy-start.18 = (bf16[8,64,2,256]{3,1,2,0:T(8,128)(2,1)}, bf16[8,64,2,256]{3,1,2,0:T(8,128)(2,1)S(1)}, u32[]{:S(2)}) copy-start(bf16[8,64,2,256]{3,1,2,0:T(8,128)(2,1)S(1)} %convolution_convert_fusion.5) | copy-start | bytes 1572868
  154.3 4.7 copy-start.72
  154.3 5.3 copy-start.20
  154.3 98.8 %all-to-all-start = ((bf16[8,4,64,1024]{3,2,1,0:T(8,128)(2,1)}), bf16[8,4,64,1024]{3,2,1,0:T(8,128)(2,1)}, u32[]{:S(2)}, u32[]{:S(2)}) async-start(bf16[8,4,64,1024]{3,2,1,0:T(8,128)(2,1)} %bitcast.509), calls=%async_computation | async-start | bytes 8388608 | tf_op jit(solution)/shard_map/all_to_all | solution.py:168
  181.4 14.3 %copy-start.24 = (f32[256,8]{1,0:T(8,128)}, f32[256,8]{1,0:T(8,128)S(1)}, u32[]{:S(2)}) copy-start(f32[256,8]{1,0:T(8,128)S(1)} %copy.166) | copy-start | bytes 24580
  253.1 98.6 %all-to-all-start.2 = ((bf16[8,4,64,1024]{3,2,1,0:T(8,128)(2,1)}), bf16[8,4,64,1024]{3,2,1,0:T(8,128)(2,1)}, u32[]{:S(2)}, u32[]{:S(2)}) async-start(bf16[8,4,64,1024]{3,2,1,0:T(8,128)(2,1)} %multiply_convert_fusion), calls=%async_computation.2 | async-start | bytes 8388608 | tf_op jit(solution)/shard_map/all_to_all | solution.py:199
  257.7 5.9 copy-start.14
  263.7 6.1 copy-start.76
  263.7 6.1 copy-start.73
  351.7 99.0 %all-to-all-start.1 = ((bf16[8,4,64,1024]{3,2,1,0:T(8,128)(2,1)}), bf16[8,4,64,1024]{3,2,1,0:T(8,128)(2,1)}, u32[]{:S(2)}, u32[]{:S(2)}) async-start(bf16[8,4,64,1024]{3,2,1,0:T(8,128)(2,1)} %copy.172), calls=%async_computation.1 | async-start | bytes 8388608 | tf_op jit(solution)/shard_map/all_to_all | solution.py:183
  356.7 4.7 copy-start.74
  363.5 5.6 copy-start.9
  363.5 6.3 copy-start.15
  369.0 3.1 copy-start.51
  369.0 3.8 copy-start.42
  369.0 4.6 copy-start.53
  369.0 5.3 copy-start.40
  378.2 77.1 %copy-start.71 = (pred[256]{0:T(512)(128)(4,1)S(1)}, pred[256]{0:T(512)(128)(4,1)}, u32[]{:S(2)}) copy-start(pred[256]{0:T(512)(128)(4,1)} %copy-done.70) | copy-start | bytes 772
  450.7 98.5 %all-to-all-start.3 = ((bf16[8,4,64,1024]{3,2,1,0:T(8,128)(2,1)}), bf16[8,4,64,1024]{3,2,1,0:T(8,128)(2,1)}, u32[]{:S(2)}, u32[]{:S(2)}) async-start(bf16[8,4,64,1024]{3,2,1,0:T(8,128)(2,1)} %copy.179), calls=%async_computation.3 | async-start | bytes 8388608 | tf_op jit(solution)/shard_map/all_to_all | solution.py:244
  455.2 176.7 %reduce-scatter.10.cloned.1.call-start = ((), (), s32[]{:S(2)}) async-start(), calls=%async_computation.15 | async-start | bytes 1310720 | tf_op jit(solution)/shard_map/reduce_scatter | solution.py:331
  460.2 14.0 %copy-start.5 = (f32[256,1024]{1,0:T(8,128)S(1)}, f32[256,1024]{1,0:T(8,128)}, u32[]{:S(2)}) copy-start(f32[256,1024]{1,0:T(8,128)} %copy-done.4) | copy-start | bytes 3145732
  474.2 7.1 copy-start.60
  474.2 7.1 copy-start.61
  474.2 7.1 copy-start.66
  567.6 5.6 copy-start.39
  567.6 5.6 copy-start.63
  567.6 6.2 copy-start.13
  567.6 6.2 copy-start.21
  567.6 6.2 copy-start.68
  575.9 3.5 copy-start.58
  576.1 5.2 copy-start.27
  579.4 5.6 copy-start.36
  581.0 57.3 %reduce-scatter.8.cloned.1.call-start = ((), (), s32[]{:S(2)}) async-start(), calls=%async_computation.14 | async-start | bytes 1310720 | tf_op jit(solution)/shard_map/reduce_scatter | solution.py:328
  581.3 3.7 copy-start.1
  588.5 3.8 copy-start.16
  590.1 86.4 %reduce-scatter.12.cloned.1.call-start = ((), (), s32[]{:S(2)}) async-start(), calls=%async_computation.16 | async-start | bytes 2621440 | tf_op jit(solution)/shard_map/reduce_scatter | solution.py:334
  592.3 3.2 copy-start.23
  592.3 122.9 %reduce-scatter.6.cloned.1.call-start = ((), (), s32[]{:S(2)}) async-start(), calls=%async_computation.13 | async-start | bytes 2621440 | tf_op jit(solution)/shard_map/reduce_scatter | solution.py:325
  598.9 143.7 %reduce-scatter.14.cloned.1.call-start = ((), (), s32[]{:S(2)}) async-start(), calls=%async_computation.17 | async-start | bytes 81920 | tf_op jit(solution)/shard_map/reduce_scatter | solution.py:340
  598.9 3.2 copy-start.52
  611.2 3.1 copy-start.44
  611.2 6.2 copy-start.79
  614.3 3.1 copy-start.77
  628.8 86.5 %copy-start.41 = (bf16[8,64,512]{2,1,0:T(8,128)(2,1)S(1)}, bf16[8,64,512]{2,1,0:T(8,128)(2,1)}, u32[]{:S(2)}) copy-start(bf16[8,64,512]{2,1,0:T(8,128)(2,1)} %copy-done.40) | copy-start | bytes 1572868
  628.8 178.8 %all-reduce.13.cloned.1.call-start = ((), (), s32[]{:S(2)}) async-start(), calls=%async_computation.18 | async-start | bytes 3145728 | tf_op jit(solution)/shard_map/psum | solution.py:346
  715.3 335.4 %all-reduce.15.cloned.1.call-start = ((), (), s32[]{:S(2)}) async-start(), calls=%async_computation.19 | async-start | bytes 25165824 | tf_op jit(solution)/shard_map/psum | solution.py:239
  717.8 3.4 copy-start.35
  723.5 5.9 copy-start.17
  725.4 4.0 copy-start.12
  1050.6 6.9 copy-start.11
  1057.6 4.6 copy-start.10
  (31 other events, 60.3 us)
Sparse Core Ops, SparseCore 0:
  9.9 29.2 all-gather.6
  41.0 26.4 all-gather.8
  69.4 35.1 all-gather.10
  106.3 35.1 all-gather.12
  581.1 25.8 reduce-scatter.9
  610.3 27.9 reduce-scatter.7
  641.3 35.1 reduce-scatter.11
  680.0 35.1 reduce-scatter.5
  718.5 24.0 reduce-scatter.13
  745.1 62.4 all-reduce.12
  812.1 238.5 all-reduce.14
where the time goes:
time: 1080 us; the launch traced here: 1070 us
  waiting for transfers between devices  706 us (65%)
  local copies, waits for them, and re-layouts  99.1 us (9%)
  matrix products  97.9 us (9%)
  other arithmetic  70.4 us (7%)
  blocking collectives  64.2 us (6%)
  starting transfers between devices  19.5 us (2%)
  between operations  16.4 us (2%)
    psum x1, waiting for transfers between devices, per_device(): lax.psum(expert_sums[0].astype(jnp.bfloat16), 'shard').astype(jnp.float32)  235 us
    all_to_all x1, waiting for transfers between devices, per_device(): lax.all_to_all(slot_grads, 'expert', split_axis=0, concat_axis=0, tiled=T...  77 us
    all_to_all x1, waiting for transfers between devices, per_device(): lax.all_to_all(results[0], 'expert', split_axis=0, concat_axis=0, tiled=T...  72.5 us
    all_to_all x1, waiting for transfers between devices, per_device(): lax.all_to_all(grads_home, 'expert', split_axis=0, concat_axis=0, tiled=T...  67.8 us
    all_to_all x1, waiting for transfers between devices, per_device(): lax.all_to_all(send_rows, 'expert', split_axis=0, concat_axis=0, tiled=True)  57.4 us
    reduce_scatter x1, waiting for transfers between devices, per_device(): lax.psum_scatter(mixer_terms[1].astype(jnp.bfloat16), 'shard', scatter_di...  38.8 us
    reduce_scatter x1, waiting for transfers between devices, per_device(): lax.psum_scatter(mixer_terms[4].astype(jnp.bfloat16), 'shard', scatter_di...  38.2 us
    psum x1, waiting for transfers between devices, per_device(): lax.psum(mixer_part[1].astype(jnp.bfloat16), 'expert').astype(jnp.float32)  34.2 us
  transfers between devices with their start and end apart: 15, of which 13 were waited for; matrix products, arithmetic and copies ran while one was open for 19% of the time, Pallas kernels for 0%

commit v1 on v0

v1 whole, which is shorter than its diff:
```python
import jax
import jax.numpy as jnp
from jax import lax
from jax.sharding import PartitionSpec as P

HEADS = 16
KV_HEADS = 8
HEAD = 64

eps = 1e-05
masked = -1e30
f32 = jnp.float32
bf16 = jnp.bfloat16


def mm(spec, a, b):
    return jnp.einsum(spec, a, b, preferred_element_type=f32)


def rope_tables(segments, head_size):
    length = segments.shape[0]
    positions = jnp.arange(length, dtype=jnp.int32)
    doc_start = jnp.sum((segments[None, :] < segments[:, None]).astype(jnp.int32), -1)
    places = (positions - doc_start).astype(f32)
    half_size = head_size // 2
    frequency = 10000.0 ** (-jnp.arange(half_size, dtype=f32) * 2.0 / head_size)
    angles = places[:, None] * frequency[None, :]
    cosine = jnp.concatenate([jnp.cos(angles), jnp.cos(angles)], -1)
    sine_table = jnp.concatenate([jnp.sin(angles), jnp.sin(angles)], -1)
    return (cosine, sine_table)


def rotate(values, cosine, sine_table):
    half_size = values.shape[-1] // 2
    turned = jnp.concatenate([-values[..., half_size:], values[..., :half_size]], -1)
    return values * cosine[:, None, :] + turned * sine_table[:, None, :]


def unrotate(grads, cosine, sine_table):
    half_size = grads.shape[-1] // 2
    scaled = grads * sine_table[:, None, :]
    turned = jnp.concatenate([scaled[..., half_size:], -scaled[..., :half_size]], -1)
    return grads * cosine[:, None, :] + turned


def allowed_mask(segments, live_int):
    length = segments.shape[0]
    rows_idx = jnp.arange(length, dtype=jnp.int32)[:, None]
    cols_idx = jnp.arange(length, dtype=jnp.int32)[None, :]
    same_doc = segments[:, None] == segments[None, :]
    return same_doc & (cols_idx <= rows_idx) & (live_int[None, :] > 0) | (cols_idx == rows_idx)


def norm_back(grad_in, normed, factor):
    return factor * (grad_in - normed * jnp.mean(grad_in * normed, -1, keepdims=True))


class Net:
    def __init__(self, owners, shards):
        self.owners, self.shards, self.levels = owners, shards, owners // 2
        self.square = shards == 4
        place = lax.axis_index("expert")
        self.owner, self.core, self.level = place, place % 2, place // 2
        self.shard = lax.axis_index("shard")

    def swap(self, x):
        return lax.ppermute(x, "expert", [(i, i ^ 1) for i in range(self.owners)])

    def lift(self, x, by):
        return lax.ppermute(
            x, "expert", [(i, (i + 2 * by) % self.owners) for i in range(self.owners)]
        )

    def flip(self, x, bits):
        return lax.ppermute(x, "shard", [(i, i ^ bits) for i in range(self.shards)])

    def over_expert(self, x):
        mine = jnp.stack([x] + [self.lift(x, k) for k in range(1, self.levels)])
        return mine, self.swap(mine)

    def home(self, mine, other):
        both = mine + self.swap(other.astype(bf16)).astype(f32)
        total = both[0]
        for k in range(1, self.levels):
            total = total + self.lift(both[k].astype(bf16), self.levels - k).astype(f32)
        return total

    def over_square(self, x):
        half = x.shape[0] // 2
        one, two = self.flip(x, 1), self.flip(x, 2)
        three = jnp.concatenate([self.flip(two[:half], 1), self.flip(one[half:], 2)], 0)
        return one, two, three

    def gather_rows(self, x):
        if not self.square:
            return lax.all_gather(x, "shard", axis=0, tiled=True)
        rows = x.shape[0] // 2
        half = lax.dynamic_slice_in_dim(x, self.core * rows, rows, 0)
        rel = jnp.stack((half,) + self.over_square(half))
        other = self.swap(rel)
        low = jnp.where(self.core == 0, rel, other)
        high = jnp.where(self.core == 0, other, rel)
        full = jnp.stack([low, high], 1)
        full = full[jnp.arange(self.shards) ^ self.shard]
        return full.reshape((self.shards * x.shape[0],) + x.shape[1:])

    def sum_rows(self, x):
        if not self.square:
            part = lax.psum_scatter(x.astype(bf16), "shard", scatter_dimension=0, tiled=True)
            return lax.psum(part, "expert").astype(f32)
        rows = x.shape[0] // self.shards // 2
        wide = x.shape[1]
        blocks = x.reshape(self.shards, 2, rows, wide)[jnp.arange(self.shards) ^ self.shard]
        mine = lax.dynamic_index_in_dim(blocks, self.core, 1, False)
        other = lax.dynamic_index_in_dim(blocks, 1 - self.core, 1, False)
        chip = mine + self.swap(other.astype(bf16)).astype(f32)
        cut = wide // 256 * 128
        ends = []
        for part, first, second in ((chip[..., :cut], 1, 2), (chip[..., cut:], 2, 1)):
            near, far = self.flip(part[first].astype(bf16), first), self.flip(part[3].astype(bf16), first)
            last = self.flip((part[second] + far.astype(f32)).astype(bf16), second)
            ends.append(part[0] + near.astype(f32) + last.astype(f32))
        own = jnp.concatenate(ends, 1)
        levels = self.levels
        parts = own.reshape(levels, rows // levels, wide)
        part_of = lambda at: lax.dynamic_index_in_dim(parts, at % levels, 0, False)
        total = part_of(self.level)
        for k in range(1, levels):
            total = total + self.lift(part_of(self.level + k).astype(bf16), k).astype(f32)
        total = total.astype(bf16)
        found = jnp.stack([total] + [self.lift(total, k) for k in range(1, levels)])
        found = found[(self.level - jnp.arange(levels)) % levels].reshape(rows, wide)
        twin = self.swap(found)
        low = jnp.where(self.core == 0, found, twin)
        high = jnp.where(self.core == 0, twin, found)
        return jnp.concatenate([low, high], 0).astype(f32)


def per_device(
    hidden_in,
    segment_ids,
    pad_mask,
    expert_choice,
    slot_rank,
    attn_gain,
    query_weight,
    key_weight,
    value_weight,
    output_weight,
    moe_gain,
    router_weight,
    gate_weight,
    up_weight,
    down_weight,
    out_grad,
):
    owners, shards = lax.axis_size("expert"), lax.axis_size("shard")
    net = Net(owners, shards)
    hidden = hidden_in[0].astype(f32)
    length, width = hidden.shape
    segments = segment_ids[0]
    live_int = pad_mask[0]
    live = live_int.astype(f32)
    choices = expert_choice[0]
    ranks = slot_rank[0]
    top_count = choices.shape[1]
    local_experts = gate_weight.shape[0]
    experts_all = owners * local_experts
    capacity = length * top_count // experts_all
    slots = local_experts * capacity
    kv_groups = HEADS // KV_HEADS
    score_scale = HEAD ** (-0.5)
    heads_wide, kv_wide = HEADS * HEAD, KV_HEADS * HEAD

    ids = jnp.arange(experts_all, dtype=jnp.int32)
    picked = jnp.any(choices.T[:, None, :] == ids[None, :, None], 0)
    active = (picked & (live_int > 0)[None, :]).astype(bf16)
    earlier = (ranks[:, None] < ranks[None, :]).astype(bf16)
    places = mm("et,tu->eu", active, earlier)
    kept = picked & (live_int > 0)[None, :] & (places < capacity)
    codes = jnp.where(kept, places, -1.0).astype(bf16)

    tail_wide = local_experts * length

    def tail_row(values):
        return jnp.pad(values.reshape(-1, tail_wide), ((0, 0), (0, width - tail_wide)))

    def with_tail(rows, first, second):
        return jnp.concatenate([rows, tail_row(first), tail_row(second)], 0)

    grad_two = (live[:, None] * out_grad[0].astype(f32)).astype(bf16)
    grad_block = with_tail(grad_two, codes, jnp.zeros_like(codes))
    grad_mine, grad_other = net.over_expert(grad_block)

    misc = jnp.concatenate(
        [router_weight, attn_gain[:, None], moe_gain[:, None]], 1
    )
    misc = jnp.pad(misc, ((0, 0), (0, 128 - misc.shape[1])))
    full = net.gather_rows(
        jnp.concatenate([query_weight, key_weight, value_weight, output_weight, misc], 1)
    )
    cuts = [heads_wide, heads_wide + kv_wide, heads_wide + 2 * kv_wide]
    query_full, key_full, value_full, output_full, misc = jnp.split(
        full, cuts + [cuts[-1] + width], 1
    )
    router_full = misc[:, :experts_all]
    gain_one = misc[:, experts_all].astype(f32)
    gain_two = misc[:, experts_all + 1].astype(f32)

    inv_one = lax.rsqrt(jnp.mean(hidden * hidden, -1, keepdims=True) + eps)
    normed_one = hidden * inv_one
    attn_in = (normed_one * gain_one).astype(bf16)
    cosine, sine_table = rope_tables(segments, HEAD)
    query_raw = jnp.dot(attn_in, query_full, preferred_element_type=f32)
    query_rot = (
        rotate(query_raw.reshape(length, HEADS, HEAD), cosine, sine_table)
        .astype(bf16)
        .reshape(length, KV_HEADS, kv_groups, HEAD)
    )
    key_raw = jnp.dot(attn_in, key_full, preferred_element_type=f32)
    key_rot = rotate(key_raw.reshape(length, KV_HEADS, HEAD), cosine, sine_table).astype(bf16)
    value_rows = (
        jnp.dot(attn_in, value_full, preferred_element_type=f32)
        .astype(bf16)
        .reshape(length, KV_HEADS, HEAD)
    )
    allowed = allowed_mask(segments, live_int)

    def score_block():
        raw_scores = mm("qgrd,kgd->grqk", query_rot, key_rot) * score_scale
        return jnp.where(allowed[None, None], raw_scores, masked)

    scores = score_block()
    top_score = jnp.max(scores, -1, keepdims=True)
    log_total = top_score + jnp.log(jnp.sum(jnp.exp(scores - top_score), -1, keepdims=True))
    probs = jnp.exp(scores - log_total)
    mixed = mm("grqk,kgd->qgrd", probs.astype(bf16), value_rows)
    attn_out = mixed.astype(bf16).reshape(length, heads_wide)
    resid_one = hidden + jnp.dot(attn_out, output_full, preferred_element_type=f32)
    inv_two = lax.rsqrt(jnp.mean(resid_one * resid_one, -1, keepdims=True) + eps)
    normed_two = resid_one * inv_two
    moe_in = (normed_two * gain_two).astype(bf16)
    logits = mm("de,td->et", router_full, moe_in)
    top_logit = jnp.max(jnp.where(picked, logits, masked), 0, keepdims=True)
    powers = jnp.where(picked, jnp.exp(jnp.minimum(logits - top_logit, 0.0)), 0.0)
    gates = powers / jnp.sum(powers, 0, keepdims=True)
    gates_kept = jnp.where(kept, gates, 0.0)
    gates_high = gates_kept.astype(bf16)
    gates_low = (gates_kept - gates_high.astype(f32)).astype(bf16)
    row_block = with_tail(moe_in, gates_high, gates_low)
    rows_mine, rows_other = net.over_expert(row_block)

    own_row = (jnp.arange(owners) == net.owner).astype(f32)

    def tail_of(block, at):
        rows = block[:, length + at * owners : length + (at + 1) * owners].astype(f32)
        row = jnp.sum(rows * own_row[None, :, None], 1)[:, :tail_wide]
        return row.reshape(-1, local_experts, 1, length)

    def column(rows, grads, data_path):
        count = rows.shape[0]
        code = tail_of(grads, 0)
        gate = tail_of(rows, 0) + tail_of(rows, 1)
        slot_ids = jnp.arange(capacity, dtype=jnp.int32).astype(f32)[None, None, :, None]
        hot = code == slot_ids
        slot_gate = jnp.sum(jnp.where(hot, gate, 0.0), -1, keepdims=True)
        pick = hot.astype(bf16).reshape(count, slots, length)
        shape = (count, local_experts, capacity, width)
        taken = mm("sqt,std->sqd", pick, rows[:, :length]).astype(bf16).reshape(shape)
        grad_rows = mm("sqt,std->sqd", pick, grads[:, :length]).astype(bf16).reshape(shape)
        gate_pre = mm("secd,edf->secf", taken, gate_weight)
        up_pre = mm("secd,edf->secf", taken, up_weight)
        sigma = jax.nn.sigmoid(gate_pre)
        silu_vals = gate_pre * sigma
        act = (silu_vals * up_pre).astype(bf16)
        raw_grads = mm("secd,efd->secf", grad_rows, down_weight)
        act_grads = raw_grads * slot_gate
        gate_pre_grads = (act_grads * up_pre * sigma * (1.0 + gate_pre * (1.0 - sigma))).astype(bf16)
        up_pre_grads = (act_grads * silu_vals).astype(bf16)
        act_scaled = (act.astype(f32) * slot_gate).astype(bf16)
        terms = (
            mm("secd,secf->edf", taken, gate_pre_grads),
            mm("secd,secf->edf", taken, up_pre_grads),
            mm("secf,secd->efd", act_scaled, grad_rows),
        )
        if not data_path:
            return terms
        gate_grads = jnp.sum(act.astype(f32) * raw_grads, -1, keepdims=True)
        gate_grads = jnp.sum(jnp.where(hot, gate_grads, 0.0), 2)
        gate_grads = tail_row(gate_grads).reshape(count, 1, width) * own_row[None, :, None]
        high = gate_grads.astype(bf16)
        low = (gate_grads - high.astype(f32)).astype(bf16)
        outs = mm("secf,efd->secd", act, down_weight)
        outs = (outs * slot_gate).astype(bf16).reshape(count, slots, width)
        branch = mm("sqt,sqd->std", pick, outs)
        back = mm("secf,edf->secd", gate_pre_grads, gate_weight)
        back = (back + mm("secf,edf->secd", up_pre_grads, up_weight)).astype(bf16)
        back = mm("sqt,sqd->std", pick, back.reshape(count, slots, width))
        back = jnp.concatenate([back, high.astype(f32), low.astype(f32)], 1)
        return terms, branch, back

    rows_all = jnp.concatenate([rows_mine, rows_other], 0)
    grads_all = jnp.concatenate([grad_mine, grad_other], 0)
    terms, branch, back = column(rows_all, grads_all, True)
    levels = net.levels
    back = net.home(back[:levels], back[levels:])
    branch = net.home(branch[:levels], branch[levels:])
    if net.square:
        near_rows, near_grads = net.over_square(rows_mine), net.over_square(grad_mine)
        for rows, grads in zip(near_rows, near_grads):
            rows = jnp.concatenate([rows, net.swap(rows)], 0)
            grads = jnp.concatenate([grads, net.swap(grads)], 0)
            more = column(rows, grads, False)
            terms = tuple(a + b for a, b in zip(terms, more))
    else:
        terms = tuple(lax.psum(a.astype(bf16), "shard").astype(f32) for a in terms)

    block_out = (live[:, None] * (resid_one + branch)).astype(bf16)
    gate_grads = back[length : length + owners] + back[length + owners :]
    gate_grads = gate_grads[:, :tail_wide].reshape(experts_all, length)
    gate_inner = jnp.sum(gates * gate_grads, 0, keepdims=True)
    logit_grads = (gates * (gate_grads - gate_inner)).astype(bf16)
    router_grad = mm("td,et->de", moe_in, logit_grads)
    moe_in_grads = back[:length] + mm("et,de->td", logit_grads, router_full)
    gain_two_grad = jnp.sum(moe_in_grads * normed_two, 0)
    resid_grad = grad_two.astype(f32) + norm_back(moe_in_grads * gain_two, normed_two, inv_two)
    branch_grad = resid_grad.astype(bf16)
    output_grad_w = mm("lh,ld->hd", attn_out, branch_grad)
    mixed_grad = mm("ld,hd->lh", branch_grad, output_full)
    mixed_grad = mixed_grad.astype(bf16).reshape(length, KV_HEADS, kv_groups, HEAD)
    probs_again = jnp.exp(score_block() - log_total)
    prob_grads = mm("qgrd,kgd->grqk", mixed_grad, value_rows)
    value_grad = mm("grqk,qgrd->kgd", probs_again.astype(bf16), mixed_grad)
    value_grad = value_grad.astype(bf16).reshape(length, kv_wide)
    score_grads = (
        probs_again * (prob_grads - jnp.sum(probs_again * prob_grads, -1, keepdims=True))
    ).astype(bf16)
    query_rot_grad = mm("grqk,kgd->qgrd", score_grads, key_rot) * score_scale
    key_rot_grad = mm("grqk,qgrd->kgd", score_grads, query_rot) * score_scale
    query_grad = (
        unrotate(query_rot_grad.reshape(length, HEADS, HEAD), cosine, sine_table)
        .astype(bf16)
        .reshape(length, heads_wide)
    )
    key_grad = unrotate(key_rot_grad, cosine, sine_table).astype(bf16).reshape(length, kv_wide)
    query_grad_w = mm("ld,lh->dh", attn_in, query_grad)
    key_grad_w = mm("ld,lh->dh", attn_in, key_grad)
    value_grad_w = mm("ld,lh->dh", attn_in, value_grad)
    attn_in_grads = mm("lh,dh->ld", query_grad, query_full)
    attn_in_grads = attn_in_grads + mm("lh,dh->ld", key_grad, key_full)
    attn_in_grads = attn_in_grads + mm("lh,dh->ld", value_grad, value_full)
    gain_one_grad = jnp.sum(attn_in_grads * normed_one, 0)
    hidden_grad = resid_grad + norm_back(attn_in_grads * gain_one, normed_one, inv_one)
    misc_grad = jnp.concatenate([router_grad, gain_one_grad[:, None], gain_two_grad[:, None]], 1)
    misc_grad = jnp.pad(misc_grad, ((0, 0), (0, 128 - misc_grad.shape[1])))
    sums = net.sum_rows(
        jnp.concatenate([query_grad_w, key_grad_w, value_grad_w, output_grad_w, misc_grad], 1)
    )
    sum_query, sum_key, sum_value, sum_output, sum_misc = jnp.split(
        sums, cuts + [cuts[-1] + width], 1
    )
    return (
        block_out[None],
        hidden_grad.astype(bf16)[None],
        sum_misc[:, experts_all],
        sum_query,
        sum_key,
        sum_value,
        sum_output,
        sum_misc[:, experts_all + 1],
        sum_misc[:, :experts_all],
        terms[0],
        terms[1],
        terms[2],
    )


def solution(mesh):
    tokens = ("expert", "shard")
    in_specs = (
        P(tokens, None, None),
        P(tokens, None),
        P(tokens, None),
        P(tokens, None, None),
        P(tokens, None),
        P("shard"),
        P("shard", None),
        P("shard", None),
        P("shard", None),
        P("shard", None),
        P("shard"),
        P("shard", None),
        P("expert", None, None),
        P("expert", None, None),
        P("expert", None, None),
        P(tokens, None, None),
    )
    out_specs = (
        P(tokens, None, None),
        P(tokens, None, None),
        P("shard"),
        P("shard", None),
        P("shard", None),
        P("shard", None),
        P("shard", None),
        P("shard"),
        P("shard", None),
        P("expert", None, None),
        P("expert", None, None),
        P("expert", None, None),
    )
    return jax.shard_map(
        per_device, mesh=mesh, in_specs=in_specs, out_specs=out_specs, check_vma=False
    )
```

time: 1080 us -> 820 us (0.76)
  waiting for transfers between devices: 706 us -> 295 us
  matrix products: 97.9 us -> 258 us
  blocking collectives: 64.2 us -> 0 us
  starting transfers between devices: 19.5 us -> 71.3 us
  local copies, waits for them, and re-layouts: 99.1 us -> 121 us
  between operations: 16.4 us -> 3.26 us
    ppermute x0 -> x49, waiting for transfers between devices: none -> 295 us  [the longest x18 153 us: lift(): lax.ppermute(x, 'expert', [(i, (i + 2 * by) % self.owners) for i in range...]
    all_to_all x4 -> x0, waiting for transfers between devices: 275 us -> none  [the longest x1 77 us: per_device(): lax.all_to_all(slot_grads, 'expert', split_axis=0, concat_axis=0, tiled=T...]
    psum x2 -> x0, waiting for transfers between devices: 269 us -> none  [the longest x1 235 us: per_device(): lax.psum(expert_sums[0].astype(jnp.bfloat16), 'shard').astype(jnp.float32)]
    dot_general x48 -> x59, matrix products: 97.9 us -> 258 us  [the longest x55 248 us: mm(): return jnp.einsum(spec, a, b, preferred_element_type=f32)]
    reduce_scatter x5 -> x0, waiting for transfers between devices: 85 us -> none  [the longest x1 38.8 us: per_device(): lax.psum_scatter(mixer_terms[1].astype(jnp.bfloat16), 'shard', scatter_di...]
    all_gather x4 -> x0, waiting for transfers between devices: 74.2 us -> none  [the longest x1 32.9 us: per_device(): lax.all_gather(query_weight, 'shard', axis=0, tiled=True)]
    ppermute x0 -> x49, starting transfers between devices: none -> 71.3 us  [the longest x18 47.6 us: lift(): lax.ppermute(x, 'expert', [(i, (i + 2 * by) % self.owners) for i in range...]
    unnamed x165 -> x277, local copies, waits for them, and re-layouts: 10.1 us -> 48.3 us
  transfers between devices with their start and end apart: 15 -> 49, of which waited for: 13 -> 24; matrix products, arithmetic and copies ran while one was open for 19% -> 29% of each run, Pallas kernels for 0% -> 0%
where the time goes in v1:
time: 820 us; the launch traced here: 810 us
  waiting for transfers between devices  295 us (36%)
  matrix products  258 us (31%)
  local copies, waits for them, and re-layouts  121 us (15%)
  starting transfers between devices  71.3 us (9%)
  other arithmetic  61.3 us (7%)
    dot_general x55, matrix products, mm(): return jnp.einsum(spec, a, b, preferred_element_type=f32)  248 us
    ppermute x18, waiting for transfers between devices, lift(): lax.ppermute(x, 'expert', [(i, (i + 2 * by) % self.owners) for i in range...  153 us
    ppermute x18, waiting for transfers between devices, flip(): return lax.ppermute(x, 'shard', [(i, i ^ bits) for i in range(self.shards)])  141 us
    unnamed x277, local copies, waits for them, and re-layouts  48.3 us
    ppermute x18, starting transfers between devices, lift(): lax.ppermute(x, 'expert', [(i, (i + 2 * by) % self.owners) for i in range...  47.6 us
    ppermute x18, starting transfers between devices, flip(): return lax.ppermute(x, 'shard', [(i, i ^ bits) for i in range(self.shards)])  22.8 us
  transfers between devices with their start and end apart: 49, of which 24 were waited for; matrix products, arithmetic and copies ran while one was open for 29% of the time, Pallas kernels for 0%

profile of v1, /device:TPU:0, one launch (start us, length us, event | category | flops | bytes accessed | tf_op | source)
XLA Modules:
  0.0 809.6 jit_solution(10189423360101411496)
XLA Ops:
  11.6 16.7 %collective-permute-done = bf16[128,3200]{1,0:T(8,128)(2,1)S(1)} collective-permute-done((bf16[128,3200]{1,0:T(8,128)(2,1)S(1)}, bf16[128,3200]{1,0:T(8,128)(2,1)S(1)}, u32[]{:S(2)}, u32[]{:S(2)}) %collective-permute-start) | collective-permute-done | bytes 819232 | tf_op jit(solution)/shard_map/ppermute | solution.py:75
  33.1 6.0 collective-permute-done.3
  54.6 31.5 %collective-permute-done.6 = bf16[272,1024]{1,0:T(8,128)(2,1)} collective-permute-done((bf16[272,1024]{1,0:T(8,128)(2,1)}, bf16[272,1024]{1,0:T(8,128)(2,1)}, u32[]{:S(2)}, u32[]{:S(2)}) %collective-permute-start.6) | collective-permute-done | bytes 557088 | tf_op jit(solution)/shard_map/ppermute | solution.py:70
  93.9 3.4 pad_maximum_fusion.1
  97.3 6.8 gather_fusion
  137.3 12.9 %collective-permute-start.10 = (bf16[272,1024]{1,0:T(8,128)(2,1)S(1)}, bf16[272,1024]{1,0:T(8,128)(2,1)S(1)}, u32[]{:S(2)}, u32[]{:S(2)}) collective-permute-start(bf16[272,1024]{1,0:T(8,128)(2,1)S(1)} %get-tuple-element.153), channel_id=1, source_target_pairs={{0,16},{4,20},{8,24},{12,28},{16,0},{20,4},{24,8},{28,12},{1,17},{... | collective-permute-start | bytes 1671176 | tf_op jit(solution)/shard_map/ppermute | solution.py:70
  150.2 4.1 collective-permute-start.11
  155.2 31.7 %collective-permute-done.10 = bf16[272,1024]{1,0:T(8,128)(2,1)S(1)} collective-permute-done((bf16[272,1024]{1,0:T(8,128)(2,1)S(1)}, bf16[272,1024]{1,0:T(8,128)(2,1)S(1)}, u32[]{:S(2)}, u32[]{:S(2)}) %collective-permute-start.10) | collective-permute-done | bytes 557088 | tf_op jit(solution)/shard_map/ppermute | solution.py:70
  195.0 10.9 %collective-permute-done.35 = bf16[4,272,1024]{2,1,0:T(8,128)(2,1)S(1)} collective-permute-done((bf16[4,272,1024]{2,1,0:T(8,128)(2,1)}, bf16[4,272,1024]{2,1,0:T(8,128)(2,1)S(1)}, u32[]{:S(2)}, u32[]{:S(2)}) %collective-permute-start.35) | collective-permute-done | bytes 2228256 | tf_op jit(solution)/shard_map/ppermute | solution.py:75
  208.4 21.5 %collective-permute-done.43 = bf16[2,272,1024]{2,1,0:T(8,128)(2,1)} collective-permute-done((bf16[2,272,1024]{2,1,0:T(8,128)(2,1)S(1)}, bf16[2,272,1024]{2,1,0:T(8,128)(2,1)}, u32[]{:S(2)}, u32[]{:S(2)}) %collective-permute-start.43) | collective-permute-done | bytes 1114144 | tf_op jit(solution)/shard_map/ppermute | solution.py:75
  231.5 10.7 %collective-permute-done.41 = bf16[4,272,1024]{2,1,0:T(8,128)(2,1)S(1)} collective-permute-done((bf16[4,272,1024]{2,1,0:T(8,128)(2,1)}, bf16[4,272,1024]{2,1,0:T(8,128)(2,1)S(1)}, u32[]{:S(2)}, u32[]{:S(2)}) %collective-permute-start.41) | collective-permute-done | bytes 2228256 | tf_op jit(solution)/shard_map/ppermute | solution.py:75
  244.6 19.3 %collective-permute-done.44 = bf16[2,272,1024]{2,1,0:T(8,128)(2,1)} collective-permute-done((bf16[2,272,1024]{2,1,0:T(8,128)(2,1)}, bf16[2,272,1024]{2,1,0:T(8,128)(2,1)}, u32[]{:S(2)}, u32[]{:S(2)}) %collective-permute-start.44) | collective-permute-done | bytes 1114144 | tf_op jit(solution)/shard_map/ppermute | solution.py:75
  266.6 11.0 %collective-permute-done.37 = bf16[4,272,1024]{2,1,0:T(8,128)(2,1)} collective-permute-done((bf16[4,272,1024]{2,1,0:T(8,128)(2,1)}, bf16[4,272,1024]{2,1,0:T(8,128)(2,1)}, u32[]{:S(2)}, u32[]{:S(2)}) %collective-permute-start.37) | collective-permute-done | bytes 2228256 | tf_op jit(solution)/shard_map/ppermute | solution.py:75
  288.7 10.7 %collective-permute-done.46 = bf16[2,272,1024]{2,1,0:T(8,128)(2,1)S(1)} collective-permute-done((bf16[2,272,1024]{2,1,0:T(8,128)(2,1)S(1)}, bf16[2,272,1024]{2,1,0:T(8,128)(2,1)S(1)}, u32[]{:S(2)}, u32[]{:S(2)}) %collective-permute-start.46) | collective-permute-done | bytes 1114144 | tf_op jit(solution)/shard_map/ppermute | solution.py:75
  299.4 6.6 collective-permute-done.47
  308.4 3.4 constant_dynamic-update-slice_fusion.19
  312.2 3.5 constant_dynamic-update-slice_fusion.18
  321.3 3.4 constant_dynamic-update-slice_fusion.21
  324.7 3.4 constant_dynamic-update-slice_fusion.26
  331.7 5.6 fusion.112
  337.4 3.4 fusion.109
  340.8 3.5 fusion.124
  357.6 4.3 fusion.57
  361.9 4.3 fusion.47
  366.1 4.5 fusion.61
  370.6 4.5 fusion.51
  375.1 4.4 fusion.59
  379.5 4.3 fusion.49
  383.8 4.4 fusion.55
  388.1 4.4 fusion.65
  392.7 10.3 %fusion.1 = (f32[8,4,64]{2,0,1:T(8,128)S(1)}, bf16[8,4,64,512]{3,2,0,1:T(8,128)(2,1)}, f32[4,8,64,512]{3,2,1,0:T(8,128)S(1)}) fusion(f32[4,8,64,512]{3,2,1,0:T(8,128)} %fusion.55, f32[4,8,64,512]{3,2,1,0:T(8,128)} %fusion.65, bf16[4,512,1024]{2,1,0:T(8,128)(2,1)} %param.30, bf16[8,4,64,1024]{3,2,1,0:T(8,128)(2,1)} %bitcast.635), kind=kOutput, calls=%fused_computation.23 | convolution fusion | flops 2156918784 | bytes 23076864 | tf_op jit(solution)/shard_map/secd,efd->secf/dot_general | solution.py:17
  405.2 9.3 %multiply_convert_fusion.4 = (bf16[8,4,64,512]{3,2,0,1:T(8,128)(2,1)}, bf16[8,4,64,512]{3,2,0,1:T(8,128)(2,1)}) fusion(f32[8,4,64]{2,0,1:T(8,128)S(1)} %copy.228, f32[4,8,64,512]{3,2,1,0:T(8,128)} %fusion.59, f32[4,8,64,512]{3,2,1,0:T(8,128)} %fusion.49, bf16[4,512,1024]{2,1,0:T(8,128)(2,1)} %param.30, bf16[8,4,64,1024]{3,2,1,0:T(8,128)(2,1)S(1)} %bitcast.674), kind=kOutput, calls=%fused_computation.140 | convolution fusion | flops 2162163712 | bytes 20979712 | tf_op jit(solution)/shard_map/secd,efd->secf/dot_general | solution.py:17
  414.5 10.6 %fusion.92 = f32[4,512,1024,1]{2,1,3,0:T(8,128)} fusion(bf16[8,4,64,1024]{3,2,1,0:T(8,128)(2,1)} %bitcast.673, f32[4,8,64,512]{3,2,1,0:T(8,128)} %fusion.49, f32[8,4,64]{2,0,1:T(8,128)S(1)} %copy.228, f32[4,8,64,512]{3,2,1,0:T(8,128)} %fusion.59), kind=kOutput, calls=%fused_computation.152 | convolution fusion | flops 2156920832 | bytes 20979712 | tf_op jit(solution)/shard_map/secf,secd->efd/dot_general | solution.py:17
  432.5 4.1 copy-done.2
  439.8 7.1 multiply_convert_fusion.5
  447.0 7.5 fusion.154
  454.5 5.8 fusion.152
  460.3 5.6 fusion.156
  468.4 4.7 fusion.3
  478.6 3.4 copy-done.39
  482.0 8.5 %multiply_convert_fusion.3 = (bf16[8,4,64,512]{3,2,0,1:T(8,128)(2,1)}, bf16[8,4,64,512]{3,2,0,1:T(8,128)(2,1)S(1)}) fusion(f32[8,4,64]{2,0,1:T(8,128)S(1)} %copy.233, f32[4,8,64,512]{3,2,1,0:T(8,128)} %fusion.57, f32[4,8,64,512]{3,2,1,0:T(8,128)} %fusion.47, bf16[4,512,1024]{2,1,0:T(8,128)(2,1)} %param.30, bf16[8,4,64,1024]{3,2,1,0:T(8,128)(2,1)S(1)} %bitcast.665), kind=kOutput, calls=%fused_computation.139 | convolution fusion | flops 2162163712 | bytes 20979712 | tf_op jit(solution)/shard_map/secd,efd->secf/dot_general | solution.py:17
  490.5 15.5 %bitcast_add_fusion.6 = f32[4,1024,512]{2,1,0:T(8,128)} fusion(f32[4,1024,512,1]{2,1,0,3:T(8,128)} %fusion.152, f32[4,1024,512,1]{2,1,0,3:T(8,128)} %fusion.154, f32[4,1024,512,1]{2,1,0,3:T(8,128)} %fusion.156, bf16[8,4,64,1024]{3,2,1,0:T(8,128)(2,1)} %bitcast.616, bf16[8,4,64,512]{3,2,0,1:T(8,128)(2,1)S(1)} %get-tuple-element.114), kind=kOutput, calls=%fused_computation.10 | convolution fusion | flops 2153775104 | bytes 39845888 | tf_op jit(solution)/shard_map/secd,secf->edf/dot_general | solution.py:17
  506.0 8.6 %fusion.149 = f32[4,1024,512,1]{2,1,0,3:T(8,128)} fusion(bf16[8,4,64,1024]{3,2,1,0:T(8,128)(2,1)} %bitcast.667, bf16[8,4,64,512]{3,2,0,1:T(8,128)(2,1)} %copy-done.15), kind=kOutput, calls=%fused_computation.198 | convolution fusion | flops 2147483648 | bytes 14680064 | tf_op jit(solution)/shard_map/secd,secf->edf/dot_general | solution.py:17
  514.6 10.8 %fusion.97 = f32[4,512,1024,1]{2,1,3,0:T(8,128)} fusion(bf16[8,4,64,1024]{3,2,1,0:T(8,128)(2,1)} %bitcast.671, f32[4,8,64,512]{3,2,1,0:T(8,128)} %fusion.51, f32[8,4,64]{2,0,1:T(8,128)S(1)} %copy.223, f32[4,8,64,512]{3,2,1,0:T(8,128)} %fusion.61), kind=kOutput, calls=%fused_computation.157 | convolution fusion | flops 2156920832 | bytes 20979712 | tf_op jit(solution)/shard_map/secf,secd->efd/dot_general | solution.py:17
  531.0 4.5 fusion.285
  539.6 16.0 %collective-permute-done.18 = bf16[272,1024]{1,0:T(8,128)(2,1)S(1)} collective-permute-done((bf16[272,1024]{1,0:T(8,128)(2,1)S(1)}, bf16[272,1024]{1,0:T(8,128)(2,1)S(1)}, u32[]{:S(2)}, u32[]{:S(2)}) %collective-permute-start.18) | collective-permute-done | bytes 557088 | tf_op jit(solution)/shard_map/ppermute | solution.py:70
  555.6 12.1 %collective-permute-start.15 = (bf16[256,1024]{1,0:T(8,128)(2,1)}, bf16[256,1024]{1,0:T(8,128)(2,1)}, u32[]{:S(2)}, u32[]{:S(2)}) collective-permute-start(bf16[256,1024]{1,0:T(8,128)(2,1)} %get-tuple-element.136), channel_id=1, source_target_pairs={{0,16},{4,20},{8,24},{12,28},{16,0},{20,4},{24,8},{28,12},{1,17},{... | collective-permute-start | bytes 1572872 | tf_op jit(solution)/shard_map/ppermute | solution.py:70
  567.7 34.9 %collective-permute-done.19 = bf16[272,1024]{1,0:T(8,128)(2,1)S(1)} collective-permute-done((bf16[272,1024]{1,0:T(8,128)(2,1)S(1)}, bf16[272,1024]{1,0:T(8,128)(2,1)S(1)}, u32[]{:S(2)}, u32[]{:S(2)}) %collective-permute-start.19) | collective-permute-done | bytes 557088 | tf_op jit(solution)/shard_map/ppermute | solution.py:70
  604.7 19.6 %collective-permute-done.15 = bf16[256,1024]{1,0:T(8,128)(2,1)} collective-permute-done((bf16[256,1024]{1,0:T(8,128)(2,1)}, bf16[256,1024]{1,0:T(8,128)(2,1)}, u32[]{:S(2)}, u32[]{:S(2)}) %collective-permute-start.15) | collective-permute-done | bytes 524320 | tf_op jit(solution)/shard_map/ppermute | solution.py:70
  630.0 3.4 fusion.178
  652.0 13.9 %copy.263 = f32[1024,3200]{1,0:T(8,128)} copy(f32[1024,3200]{0,1:T(8,128)} %fusion.218) | data formatting | bytes 26214400 | tf_op jit(solution)/shard_map/reshape | solution.py:113
  665.9 11.0 %gather_fusion.1 = f32[4,2,128,3200]{3,2,1,0:T(8,128)} fusion(f32[4,2,128,3200]{3,2,1,0:T(8,128)} %bitcast.613, s32[1024]{0:T(1024)} %copy-done.96), kind=kCustom, calls=%fused_computation.1 | custom fusion | bytes 26214416 | tf_op jit(solution)/shard_map/gather | solution.py:113
  676.9 5.1 fusion.105
  682.0 9.6 %fusion.87 = f32[4,512,1024,1]{2,1,3,0:T(8,128)} fusion(bf16[8,4,64,1024]{3,2,1,0:T(8,128)(2,1)S(1)} %bitcast.666, f32[4,8,64,512]{3,2,1,0:T(8,128)} %fusion.47, f32[8,4,64]{2,0,1:T(8,128)S(1)} %copy.233, f32[4,8,64,512]{3,2,1,0:T(8,128)} %fusion.57), kind=kOutput, calls=%fused_computation.147 | convolution fusion | flops 2156920832 | bytes 20979712 | tf_op jit(solution)/shard_map/secf,secd->efd/dot_general | solution.py:17
  691.6 16.2 %bitcast_add_fusion = f32[4,512,1024]{2,1,0:T(8,128)} fusion(f32[4,512,1024,1]{2,1,3,0:T(8,128)} %fusion.87, f32[4,512,1024,1]{2,1,3,0:T(8,128)} %fusion.92, f32[4,512,1024,1]{2,1,3,0:T(8,128)} %fusion.97, bf16[8,4,64,1024]{3,2,1,0:T(8,128)(2,1)} %bitcast.636, bf16[8,4,64,512]{3,2,0,1:T(8,128)(2,1)} %get-tuple-element.110, f32[8,4,64]{2,0,1:T(8,128)S(1)} %copy-done.81), kind=kOutput, calls=%fused_computation.4 | convolution fusion | flops 2156920832 | bytes 39854080 | tf_op jit(solution)/shard_map/secf,secd->efd/dot_general | solution.py:17
  707.8 4.7 fusion.283
  716.8 15.8 %collective-permute-done.23 = bf16[128,1536]{1,0:T(8,128)(2,1)S(1)} collective-permute-done((bf16[128,1536]{1,0:T(8,128)(2,1)S(1)}, bf16[128,1536]{1,0:T(8,128)(2,1)S(1)}, u32[]{:S(2)}, u32[]{:S(2)}) %collective-permute-start.23) | collective-permute-done | bytes 393248 | tf_op jit(solution)/shard_map/ppermute | solution.py:75
  737.7 6.3 collective-permute-done.24
  746.9 3.8 collective-permute-start.30
  750.8 5.7 fusion.147
  756.8 8.2 %collective-permute-done.29 = bf16[32,3200]{1,0:T(8,128)(2,1)S(1)} collective-permute-done((bf16[32,3200]{1,0:T(8,128)(2,1)S(1)}, bf16[32,3200]{1,0:T(8,128)(2,1)S(1)}, u32[]{:S(2)}, u32[]{:S(2)}) %collective-permute-start.29) | collective-permute-done | bytes 204832 | tf_op jit(solution)/shard_map/ppermute | solution.py:70
  767.5 5.8 fusion.145
  773.3 8.9 %collective-permute-done.32 = bf16[32,3200]{1,0:T(8,128)(2,1)S(1)} collective-permute-done((bf16[32,3200]{1,0:T(8,128)(2,1)S(1)}, bf16[32,3200]{1,0:T(8,128)(2,1)S(1)}, u32[]{:S(2)}, u32[]{:S(2)}) %collective-permute-start.32) | collective-permute-done | bytes 204832 | tf_op jit(solution)/shard_map/ppermute | solution.py:70
  786.0 16.1 %bitcast_add_fusion.3 = f32[4,1024,512]{2,1,0:T(8,128)} fusion(f32[4,1024,512,1]{2,1,0,3:T(8,128)} %fusion.145, f32[4,1024,512,1]{2,1,0,3:T(8,128)} %fusion.147, f32[4,1024,512,1]{2,1,0,3:T(8,128)} %fusion.149, bf16[8,4,64,1024]{3,2,1,0:T(8,128)(2,1)} %bitcast.617, bf16[8,4,64,512]{3,2,0,1:T(8,128)(2,1)} %get-tuple-element.113), kind=kOutput, calls=%fused_computation.7 | convolution fusion | flops 2153775104 | bytes 39845888 | tf_op jit(solution)/shard_map/secd,secf->edf/dot_general | solution.py:17
  (519 shorter events, 207.9 us)
Async XLA Ops:
  7.1 21.3 %collective-permute-start = (bf16[128,3200]{1,0:T(8,128)(2,1)S(1)}, bf16[128,3200]{1,0:T(8,128)(2,1)S(1)}, u32[]{:S(2)}, u32[]{:S(2)}) collective-permute-start(bf16[128,3200]{1,0:T(8,128)(2,1)S(1)} %constant_dynamic-slice_fusion), channel_id=1, source_target_pairs={{0,1},{1,0},{2,3},{3,2},{4,5},{5,4},{6,7},{7,6},{8,9},{9,8},{10,11... | collective-permute-start | bytes 2457608 | tf_op jit(solution)/shard_map/ppermute | solution.py:75
  10.1 20.1 %collective-permute-start.1 = (bf16[128,3200]{1,0:T(8,128)(2,1)S(1)}, bf16[128,3200]{1,0:T(8,128)(2,1)S(1)}, u32[]{:S(2)}, u32[]{:S(2)}) collective-permute-start(bf16[128,3200]{1,0:T(8,128)(2,1)S(1)} %constant_dynamic-slice_fusion), channel_id=1, source_target_pairs={{0,2},{1,3},{2,0},{3,1},{4,6},{5,7},{6,4},{7,5},{8,10},{9,11},{10,... | collective-permute-start | bytes 2457608 | tf_op jit(solution)/shard_map/ppermute | solution.py:75
  28.4 10.7 %collective-permute-start.3 = (bf16[64,3200]{1,0:T(8,128)(2,1)S(1)}, bf16[64,3200]{1,0:T(8,128)(2,1)S(1)}, u32[]{:S(2)}, u32[]{:S(2)}) collective-permute-start(bf16[64,3200]{1,0:T(8,128)(2,1)S(1)} %slice.287), channel_id=1, source_target_pairs={{0,2},{1,3},{2,0},{3,1},{4,6},{5,7},{6,4},{7,5},{8,10},{9,11},{10,... | collective-permute-start | bytes 1228808 | tf_op jit(solution)/shard_map/ppermute | solution.py:75
  30.3 10.1 %collective-permute-start.2 = (bf16[64,3200]{1,0:T(8,128)(2,1)S(1)}, bf16[64,3200]{1,0:T(8,128)(2,1)S(1)}, u32[]{:S(2)}, u32[]{:S(2)}) collective-permute-start(bf16[64,3200]{1,0:T(8,128)(2,1)S(1)} %slice.286), channel_id=1, source_target_pairs={{0,1},{1,0},{2,3},{3,2},{4,5},{5,4},{6,7},{7,6},{8,9},{9,8},{10,11... | collective-permute-start | bytes 1228808 | tf_op jit(solution)/shard_map/ppermute | solution.py:75
  42.5 49.0 %collective-permute-start.4 = (bf16[4,128,3200]{2,1,0:T(8,128)(2,1)}, bf16[4,128,3200]{2,1,0:T(8,128)(2,1)}, u32[]{:S(2)}, u32[]{:S(2)}) collective-permute-start(bf16[4,128,3200]{2,1,0:T(8,128)(2,1)} %pad_maximum_fusion.2), channel_id=1, source_target_pairs={{0,4},{4,0},{8,12},{12,8},{16,20},{20,16},{24,28},{28,24},{1,5},{5... | collective-permute-start | bytes 9830408 | tf_op jit(solution)/shard_map/ppermute | solution.py:67
  42.6 94.1 %copy-start.72 = (pred[32,256]{1,0:T(8,128)(4,1)}, pred[32,256]{1,0:T(8,128)(4,1)S(1)}, u32[]{:S(2)}) copy-start(pred[32,256]{1,0:T(8,128)(4,1)S(1)} %fusion.241) | copy-start | bytes 24580
  45.5 40.6 %collective-permute-start.6 = (bf16[272,1024]{1,0:T(8,128)(2,1)}, bf16[272,1024]{1,0:T(8,128)(2,1)}, u32[]{:S(2)}, u32[]{:S(2)}) collective-permute-start(bf16[272,1024]{1,0:T(8,128)(2,1)} %get-tuple-element.155), channel_id=1, source_target_pairs={{0,16},{4,20},{8,24},{12,28},{16,0},{20,4},{24,8},{28,12},{1,17},{... | collective-permute-start | bytes 1671176 | tf_op jit(solution)/shard_map/ppermute | solution.py:70
  48.1 38.0 %collective-permute-start.5 = (bf16[272,1024]{1,0:T(8,128)(2,1)}, bf16[272,1024]{1,0:T(8,128)(2,1)}, u32[]{:S(2)}, u32[]{:S(2)}) collective-permute-start(bf16[272,1024]{1,0:T(8,128)(2,1)} %get-tuple-element.155), channel_id=1, source_target_pairs={{0,8},{4,12},{8,16},{12,20},{16,24},{20,28},{24,0},{28,4},{1,9},{5... | collective-permute-start | bytes 1671176 | tf_op jit(solution)/shard_map/ppermute | solution.py:70
  49.6 37.5 %collective-permute-start.7 = (bf16[272,1024]{1,0:T(8,128)(2,1)}, bf16[272,1024]{1,0:T(8,128)(2,1)}, u32[]{:S(2)}, u32[]{:S(2)}) collective-permute-start(bf16[272,1024]{1,0:T(8,128)(2,1)} %get-tuple-element.155), channel_id=1, source_target_pairs={{0,24},{4,28},{8,0},{12,4},{16,8},{20,12},{24,16},{28,20},{1,25},{... | collective-permute-start | bytes 1671176 | tf_op jit(solution)/shard_map/ppermute | solution.py:70
  53.2 71.6 %copy-start.84 = (f32[256]{0:T(256)}, f32[256]{0:T(256)S(1)}, u32[]{:S(2)}) copy-start(f32[256]{0:T(256)S(1)} %add_rsqrt_fusion.1) | copy-start | bytes 3076
  90.4 101.2 %collective-permute-start.39 = (bf16[4,272,1024]{2,1,0:T(8,128)(2,1)}, bf16[4,272,1024]{2,1,0:T(8,128)(2,1)}, u32[]{:S(2)}, u32[]{:S(2)}) collective-permute-start(bf16[4,272,1024]{2,1,0:T(8,128)(2,1)} %pad_maximum_fusion.3), channel_id=1, source_target_pairs={{0,2},{1,3},{2,0},{3,1},{4,6},{5,7},{6,4},{7,5},{8,10},{9,11},{10,... | collective-permute-start | bytes 6684680 | tf_op jit(solution)/shard_map/ppermute | solution.py:75
  135.2 164.2 %copy-start.9 = (bf16[256,1024]{1,0:T(8,128)(2,1)}, bf16[256,1024]{1,0:T(8,128)(2,1)S(1)}, u32[]{:S(2)}) copy-start(bf16[256,1024]{1,0:T(8,128)(2,1)S(1)} %multiply_convert_fusion.10) | copy-start | bytes 1572868
  136.7 56.2 %copy-start.86 = (f32[256]{0:T(256)}, f32[256]{0:T(256)S(1)}, u32[]{:S(2)}) copy-start(f32[256]{0:T(256)S(1)} %get-tuple-element.178) | copy-start | bytes 3076
  136.7 56.2 %copy-start.88 = (f32[256]{0:T(256)}, f32[256]{0:T(256)S(1)}, u32[]{:S(2)}) copy-start(f32[256]{0:T(256)S(1)} %fusion.259) | copy-start | bytes 3076
  137.3 49.7 %collective-permute-start.10 = (bf16[272,1024]{1,0:T(8,128)(2,1)S(1)}, bf16[272,1024]{1,0:T(8,128)(2,1)S(1)}, u32[]{:S(2)}, u32[]{:S(2)}) collective-permute-start(bf16[272,1024]{1,0:T(8,128)(2,1)S(1)} %get-tuple-element.153), channel_id=1, source_target_pairs={{0,16},{4,20},{8,24},{12,28},{16,0},{20,4},{24,8},{28,12},{1,17},{... | collective-permute-start | bytes 1671176 | tf_op jit(solution)/shard_map/ppermute | solution.py:70
  150.2 36.8 %collective-permute-start.9 = (bf16[272,1024]{1,0:T(8,128)(2,1)S(1)}, bf16[272,1024]{1,0:T(8,128)(2,1)S(1)}, u32[]{:S(2)}, u32[]{:S(2)}) collective-permute-start(bf16[272,1024]{1,0:T(8,128)(2,1)S(1)} %get-tuple-element.153), channel_id=1, source_target_pairs={{0,8},{4,12},{8,16},{12,20},{16,24},{20,28},{24,0},{28,4},{1,9},{5... | collective-permute-start | bytes 1671176 | tf_op jit(solution)/shard_map/ppermute | solution.py:70
  150.2 38.0 %collective-permute-start.11 = (bf16[272,1024]{1,0:T(8,128)(2,1)S(1)}, bf16[272,1024]{1,0:T(8,128)(2,1)S(1)}, u32[]{:S(2)}, u32[]{:S(2)}) collective-permute-start(bf16[272,1024]{1,0:T(8,128)(2,1)S(1)} %get-tuple-element.153), channel_id=1, source_target_pairs={{0,24},{4,28},{8,0},{12,4},{16,8},{20,12},{24,16},{28,20},{1,25},{... | collective-permute-start | bytes 1671176 | tf_op jit(solution)/shard_map/ppermute | solution.py:70
  154.4 51.5 %collective-permute-start.35 = (bf16[4,272,1024]{2,1,0:T(8,128)(2,1)}, bf16[4,272,1024]{2,1,0:T(8,128)(2,1)S(1)}, u32[]{:S(2)}, u32[]{:S(2)}) collective-permute-start(bf16[4,272,1024]{2,1,0:T(8,128)(2,1)} %pad_maximum_fusion.3), channel_id=1, source_target_pairs={{0,1},{1,0},{2,3},{3,2},{4,5},{5,4},{6,7},{7,6},{8,9},{9,8},{10,11... | collective-permute-start | bytes 6684680 | tf_op jit(solution)/shard_map/ppermute | solution.py:75
  190.7 51.5 %collective-permute-start.41 = (bf16[4,272,1024]{2,1,0:T(8,128)(2,1)}, bf16[4,272,1024]{2,1,0:T(8,128)(2,1)S(1)}, u32[]{:S(2)}, u32[]{:S(2)}) collective-permute-start(bf16[4,272,1024]{2,1,0:T(8,128)(2,1)} %pad_maximum_fusion.4), channel_id=1, source_target_pairs={{0,2},{1,3},{2,0},{3,1},{4,6},{5,7},{6,4},{7,5},{8,10},{9,11},{10,... | collective-permute-start | bytes 6684680 | tf_op jit(solution)/shard_map/ppermute | solution.py:75
  192.9 36.9 %collective-permute-start.43 = (bf16[2,272,1024]{2,1,0:T(8,128)(2,1)S(1)}, bf16[2,272,1024]{2,1,0:T(8,128)(2,1)}, u32[]{:S(2)}, u32[]{:S(2)}) collective-permute-start(bf16[2,272,1024]{2,1,0:T(8,128)(2,1)S(1)} %slice.337), channel_id=1, source_target_pairs={{0,1},{1,0},{2,3},{3,2},{4,5},{5,4},{6,7},{7,6},{8,9},{9,8},{10,11... | collective-permute-start | bytes 3342344 | tf_op jit(solution)/shard_map/ppermute | solution.py:75
  194.5 83.1 %collective-permute-start.37 = (bf16[4,272,1024]{2,1,0:T(8,128)(2,1)}, bf16[4,272,1024]{2,1,0:T(8,128)(2,1)}, u32[]{:S(2)}, u32[]{:S(2)}) collective-permute-start(bf16[4,272,1024]{2,1,0:T(8,128)(2,1)} %pad_maximum_fusion.4), channel_id=1, source_target_pairs={{0,1},{1,0},{2,3},{3,2},{4,5},{5,4},{6,7},{7,6},{8,9},{9,8},{10,11... | collective-permute-start | bytes 6684680 | tf_op jit(solution)/shard_map/ppermute | solution.py:75
  195.0 83.9 %collective-permute-start.8 = (bf16[4,272,1024]{2,1,0:T(8,128)(2,1)}, bf16[4,272,1024]{2,1,0:T(8,128)(2,1)}, u32[]{:S(2)}, u32[]{:S(2)}) collective-permute-start(bf16[4,272,1024]{2,1,0:T(8,128)(2,1)} %pad_maximum_fusion.3), channel_id=1, source_target_pairs={{0,4},{4,0},{8,12},{12,8},{16,20},{20,16},{24,28},{28,24},{1,5},{5... | collective-permute-start | bytes 6684680 | tf_op jit(solution)/shard_map/ppermute | solution.py:67
  205.9 77.2 %collective-permute-start.40 = (bf16[4,272,1024]{2,1,0:T(8,128)(2,1)}, bf16[4,272,1024]{2,1,0:T(8,128)(2,1)}, u32[]{:S(2)}, u32[]{:S(2)}) collective-permute-start(bf16[4,272,1024]{2,1,0:T(8,128)(2,1)} %collective-permute-done.39), channel_id=1, source_target_pairs={{0,4},{4,0},{8,12},{12,8},{16,20},{20,16},{24,28},{28,24},{1,5},{5... | collective-permute-start | bytes 6684680 | tf_op jit(solution)/shard_map/ppermute | solution.py:67
  229.9 34.1 %collective-permute-start.44 = (bf16[2,272,1024]{2,1,0:T(8,128)(2,1)}, bf16[2,272,1024]{2,1,0:T(8,128)(2,1)}, u32[]{:S(2)}, u32[]{:S(2)}) collective-permute-start(bf16[2,272,1024]{2,1,0:T(8,128)(2,1)} %slice.338), channel_id=1, source_target_pairs={{0,2},{1,3},{2,0},{3,1},{4,6},{5,7},{6,4},{7,5},{8,10},{9,11},{10,... | collective-permute-start | bytes 3342344 | tf_op jit(solution)/shard_map/ppermute | solution.py:75
  242.2 65.6 %collective-permute-start.36 = (bf16[4,272,1024]{2,1,0:T(8,128)(2,1)}, bf16[4,272,1024]{2,1,0:T(8,128)(2,1)S(1)}, u32[]{:S(2)}, u32[]{:S(2)}) collective-permute-start(bf16[4,272,1024]{2,1,0:T(8,128)(2,1)} %copy-done.23), channel_id=1, source_target_pairs={{0,4},{4,0},{8,12},{12,8},{16,20},{20,16},{24,28},{28,24},{1,5},{5... | collective-permute-start | bytes 6684680 | tf_op jit(solution)/shard_map/ppermute | solution.py:67
  263.9 35.4 %collective-permute-start.46 = (bf16[2,272,1024]{2,1,0:T(8,128)(2,1)S(1)}, bf16[2,272,1024]{2,1,0:T(8,128)(2,1)S(1)}, u32[]{:S(2)}, u32[]{:S(2)}) collective-permute-start(bf16[2,272,1024]{2,1,0:T(8,128)(2,1)S(1)} %slice.340), channel_id=1, source_target_pairs={{0,1},{1,0},{2,3},{3,2},{4,5},{5,4},{6,7},{7,6},{8,9},{9,8},{10,11... | collective-permute-start | bytes 3342344 | tf_op jit(solution)/shard_map/ppermute | solution.py:75
  277.6 34.4 %collective-permute-start.45 = (bf16[4,272,1024]{2,1,0:T(8,128)(2,1)S(1)}, bf16[4,272,1024]{2,1,0:T(8,128)(2,1)S(1)}, u32[]{:S(2)}, u32[]{:S(2)}) collective-permute-start(bf16[4,272,1024]{2,1,0:T(8,128)(2,1)S(1)} %pad_maximum_fusion.5), channel_id=1, source_target_pairs={{0,4},{4,0},{8,12},{12,8},{16,20},{20,16},{24,28},{28,24},{1,5},{5... | collective-permute-start | bytes 6684680 | tf_op jit(solution)/shard_map/ppermute | solution.py:67
  278.9 27.0 %collective-permute-start.47 = (bf16[2,272,1024]{2,1,0:T(8,128)(2,1)S(1)}, bf16[2,272,1024]{2,1,0:T(8,128)(2,1)S(1)}, u32[]{:S(2)}, u32[]{:S(2)}) collective-permute-start(bf16[2,272,1024]{2,1,0:T(8,128)(2,1)S(1)} %slice.341), channel_id=1, source_target_pairs={{0,2},{1,3},{2,0},{3,1},{4,6},{5,7},{6,4},{7,5},{8,10},{9,11},{10,... | collective-permute-start | bytes 3342344 | tf_op jit(solution)/shard_map/ppermute | solution.py:75
  283.1 32.8 %collective-permute-start.12 = (bf16[4,272,1024]{2,1,0:T(8,128)(2,1)}, bf16[4,272,1024]{2,1,0:T(8,128)(2,1)}, u32[]{:S(2)}, u32[]{:S(2)}) collective-permute-start(bf16[4,272,1024]{2,1,0:T(8,128)(2,1)} %pad_maximum_fusion.4), channel_id=1, source_target_pairs={{0,4},{4,0},{8,12},{12,8},{16,20},{20,16},{24,28},{28,24},{1,5},{5... | collective-permute-start | bytes 6684680 | tf_op jit(solution)/shard_map/ppermute | solution.py:67
  299.4 18.6 %collective-permute-start.38 = (bf16[4,272,1024]{2,1,0:T(8,128)(2,1)}, bf16[4,272,1024]{2,1,0:T(8,128)(2,1)}, u32[]{:S(2)}, u32[]{:S(2)}) collective-permute-start(bf16[4,272,1024]{2,1,0:T(8,128)(2,1)} %collective-permute-done.37), channel_id=1, source_target_pairs={{0,4},{4,0},{8,12},{12,8},{16,20},{20,16},{24,28},{28,24},{1,5},{5... | collective-permute-start | bytes 6684680 | tf_op jit(solution)/shard_map/ppermute | solution.py:67
  306.0 15.3 %collective-permute-start.42 = (bf16[4,272,1024]{2,1,0:T(8,128)(2,1)S(1)}, bf16[4,272,1024]{2,1,0:T(8,128)(2,1)}, u32[]{:S(2)}, u32[]{:S(2)}) collective-permute-start(bf16[4,272,1024]{2,1,0:T(8,128)(2,1)S(1)} %collective-permute-done.41), channel_id=1, source_target_pairs={{0,4},{4,0},{8,12},{12,8},{16,20},{20,16},{24,28},{28,24},{1,5},{5... | collective-permute-start | bytes 6684680 | tf_op jit(solution)/shard_map/ppermute | solution.py:67
  307.7 17.0 %collective-permute-start.48 = (bf16[4,272,1024]{2,1,0:T(8,128)(2,1)}, bf16[4,272,1024]{2,1,0:T(8,128)(2,1)}, u32[]{:S(2)}, u32[]{:S(2)}) collective-permute-start(bf16[4,272,1024]{2,1,0:T(8,128)(2,1)} %pad_maximum_fusion.6), channel_id=1, source_target_pairs={{0,4},{4,0},{8,12},{12,8},{16,20},{20,16},{24,28},{28,24},{1,5},{5... | collective-permute-start | bytes 6684680 | tf_op jit(solution)/shard_map/ppermute | solution.py:67
  438.3 92.7 %collective-permute-start.13 = (bf16[4,256,1024]{2,1,0:T(8,128)(2,1)}, bf16[4,256,1024]{2,1,0:T(8,128)(2,1)}, u32[]{:S(2)}, u32[]{:S(2)}) collective-permute-start(bf16[4,256,1024]{2,1,0:T(8,128)(2,1)} %slice.462), channel_id=1, source_target_pairs={{0,4},{4,0},{8,12},{12,8},{16,20},{20,16},{24,28},{28,24},{1,5},{5... | collective-permute-start | bytes 6291464 | tf_op jit(solution)/shard_map/ppermute | solution.py:67
  478.4 46.9 %collective-permute-start.17 = (bf16[4,272,1024]{2,1,0:T(8,128)(2,1)}, bf16[4,272,1024]{2,1,0:T(8,128)(2,1)}, u32[]{:S(2)}, u32[]{:S(2)}) collective-permute-start(bf16[4,272,1024]{2,1,0:T(8,128)(2,1)} %slice.461), channel_id=1, source_target_pairs={{0,4},{4,0},{8,12},{12,8},{16,20},{20,16},{24,28},{28,24},{1,5},{5... | collective-permute-start | bytes 6684680 | tf_op jit(solution)/shard_map/ppermute | solution.py:67
  528.1 27.5 %collective-permute-start.18 = (bf16[272,1024]{1,0:T(8,128)(2,1)S(1)}, bf16[272,1024]{1,0:T(8,128)(2,1)S(1)}, u32[]{:S(2)}, u32[]{:S(2)}) collective-permute-start(bf16[272,1024]{1,0:T(8,128)(2,1)S(1)} %get-tuple-element.131), channel_id=1, source_target_pairs={{0,24},{4,28},{8,0},{12,4},{16,8},{20,12},{24,16},{28,20},{1,25},{... | collective-permute-start | bytes 1671176 | tf_op jit(solution)/shard_map/ppermute | solution.py:70
  528.2 39.5 %collective-permute-start.20 = (bf16[272,1024]{1,0:T(8,128)(2,1)S(1)}, bf16[272,1024]{1,0:T(8,128)(2,1)S(1)}, u32[]{:S(2)}, u32[]{:S(2)}) collective-permute-start(bf16[272,1024]{1,0:T(8,128)(2,1)S(1)} %get-tuple-element.132), channel_id=1, source_target_pairs={{0,8},{4,12},{8,16},{12,20},{16,24},{20,28},{24,0},{28,4},{1,9},{5... | collective-permute-start | bytes 1671176 | tf_op jit(solution)/shard_map/ppermute | solution.py:70
  530.3 72.2 %collective-permute-start.19 = (bf16[272,1024]{1,0:T(8,128)(2,1)S(1)}, bf16[272,1024]{1,0:T(8,128)(2,1)S(1)}, u32[]{:S(2)}, u32[]{:S(2)}) collective-permute-start(bf16[272,1024]{1,0:T(8,128)(2,1)S(1)} %get-tuple-element.133), channel_id=1, source_target_pairs={{0,16},{4,20},{8,24},{12,28},{16,0},{20,4},{24,8},{28,12},{1,17},{... | collective-permute-start | bytes 1671176 | tf_op jit(solution)/shard_map/ppermute | solution.py:70
  535.5 67.4 %copy-start.71 = (f32[32,256]{1,0:T(8,128)S(1)}, f32[32,256]{1,0:T(8,128)}, u32[]{:S(2)}) copy-start(f32[32,256]{1,0:T(8,128)} %copy-done.70) | copy-start | bytes 98308
  535.5 67.4 %copy-start.73 = (pred[32,256]{1,0:T(8,128)(4,1)S(1)}, pred[32,256]{1,0:T(8,128)(4,1)}, u32[]{:S(2)}) copy-start(pred[32,256]{1,0:T(8,128)(4,1)} %copy-done.72) | copy-start | bytes 24580
  535.5 67.4 %copy-start.87 = (f32[256]{0:T(256)S(1)}, f32[256]{0:T(256)}, u32[]{:S(2)}) copy-start(f32[256]{0:T(256)} %copy-done.86) | copy-start | bytes 3076
  535.5 67.4 %copy-start.89 = (f32[256]{0:T(256)S(1)}, f32[256]{0:T(256)}, u32[]{:S(2)}) copy-start(f32[256]{0:T(256)} %copy-done.88) | copy-start | bytes 3076
  535.5 67.5 %copy-start.8 = (f32[256,1024]{1,0:T(8,128)S(1)}, f32[256,1024]{1,0:T(8,128)}, u32[]{:S(2)}) copy-start(f32[256,1024]{1,0:T(8,128)} %copy-done.7) | copy-start | bytes 3145732
  535.5 67.5 %copy-start.83 = (f32[1024,1]{0,1:T(1,128)S(1)}, f32[1024,1]{0,1:T(1,128)}, u32[]{:S(2)}) copy-start(f32[1024,1]{0,1:T(1,128)} %copy-done.82) | copy-start | bytes 12292
  535.6 67.5 %copy-start.92 = (f32[256]{0:T(256)S(1)}, f32[256]{0:T(256)}, u32[]{:S(2)}) copy-start(f32[256]{0:T(256)} %copy-done.91) | copy-start | bytes 3076
  536.7 67.8 %copy-start.10 = (bf16[256,1024]{1,0:T(8,128)(2,1)S(1)}, bf16[256,1024]{1,0:T(8,128)(2,1)}, u32[]{:S(2)}) copy-start(bf16[256,1024]{1,0:T(8,128)(2,1)} %copy-done.9) | copy-start | bytes 1572868
  536.7 87.6 %copy-start.58 = (bf16[1,256,1024]{2,1,0:T(8,128)(2,1)S(1)}, bf16[1,256,1024]{2,1,0:T(8,128)(2,1)}, u32[]{:S(2)}) copy-start(bf16[1,256,1024]{2,1,0:T(8,128)(2,1)} %param.31) | copy-start | bytes 1572868
  536.7 87.6 %copy-start.94 = (f32[1,256]{1,0:T(1,128)S(1)}, f32[1,256]{1,0:T(1,128)}, u32[]{:S(2)}) copy-start(f32[1,256]{1,0:T(1,128)} %copy-done.93) | copy-start | bytes 3076
  536.7 68.0 %collective-permute-start.14 = (bf16[256,1024]{1,0:T(8,128)(2,1)}, bf16[256,1024]{1,0:T(8,128)(2,1)}, u32[]{:S(2)}, u32[]{:S(2)}) collective-permute-start(bf16[256,1024]{1,0:T(8,128)(2,1)} %get-tuple-element.134), channel_id=1, source_target_pairs={{0,24},{4,28},{8,0},{12,4},{16,8},{20,12},{24,16},{28,20},{1,25},{... | collective-permute-start | bytes 1572872 | tf_op jit(solution)/shard_map/ppermute | solution.py:70
  539.6 65.1 %collective-permute-start.16 = (bf16[256,1024]{1,0:T(8,128)(2,1)}, bf16[256,1024]{1,0:T(8,128)(2,1)}, u32[]{:S(2)}, u32[]{:S(2)}) collective-permute-start(bf16[256,1024]{1,0:T(8,128)(2,1)} %get-tuple-element.135), channel_id=1, source_target_pairs={{0,8},{4,12},{8,16},{12,20},{16,24},{20,28},{24,0},{28,4},{1,9},{5... | collective-permute-start | bytes 1572872 | tf_op jit(solution)/shard_map/ppermute | solution.py:70
  555.6 68.7 %collective-permute-start.15 = (bf16[256,1024]{1,0:T(8,128)(2,1)}, bf16[256,1024]{1,0:T(8,128)(2,1)}, u32[]{:S(2)}, u32[]{:S(2)}) collective-permute-start(bf16[256,1024]{1,0:T(8,128)(2,1)} %get-tuple-element.136), channel_id=1, source_target_pairs={{0,16},{4,20},{8,24},{12,28},{16,0},{20,4},{24,8},{28,12},{1,17},{... | collective-permute-start | bytes 1572872 | tf_op jit(solution)/shard_map/ppermute | solution.py:70
  682.0 25.8 %collective-permute-start.21 = (bf16[4,128,3200]{2,1,0:T(8,128)(2,1)}, bf16[4,128,3200]{2,1,0:T(8,128)(2,1)}, u32[]{:S(2)}, u32[]{:S(2)}) collective-permute-start(bf16[4,128,3200]{2,1,0:T(8,128)(2,1)} %fusion.105), channel_id=1, source_target_pairs={{0,4},{4,0},{8,12},{12,8},{16,20},{20,16},{24,28},{28,24},{1,5},{5... | collective-permute-start | bytes 9830408 | tf_op jit(solution)/shard_map/ppermute | solution.py:67
  712.6 25.1 %collective-permute-start.22 = (bf16[128,1536]{1,0:T(8,128)(2,1)S(1)}, bf16[128,1536]{1,0:T(8,128)(2,1)S(1)}, u32[]{:S(2)}, u32[]{:S(2)}) collective-permute-start(bf16[128,1536]{1,0:T(8,128)(2,1)S(1)} %get-tuple-element.127), channel_id=1, source_target_pairs={{0,1},{1,0},{2,3},{3,2},{4,5},{5,4},{6,7},{7,6},{8,9},{9,8},{10,11... | collective-permute-start | bytes 1179656 | tf_op jit(solution)/shard_map/ppermute | solution.py:75
  713.9 18.7 %collective-permute-start.23 = (bf16[128,1536]{1,0:T(8,128)(2,1)S(1)}, bf16[128,1536]{1,0:T(8,128)(2,1)S(1)}, u32[]{:S(2)}, u32[]{:S(2)}) collective-permute-start(bf16[128,1536]{1,0:T(8,128)(2,1)S(1)} %get-tuple-element.128), channel_id=1, source_target_pairs={{0,1},{1,0},{2,3},{3,2},{4,5},{5,4},{6,7},{7,6},{8,9},{9,8},{10,11... | collective-permute-start | bytes 1179656 | tf_op jit(solution)/shard_map/ppermute | solution.py:75
  714.7 29.4 %collective-permute-start.25 = (bf16[128,1664]{1,0:T(8,128)(2,1)S(1)}, bf16[128,1664]{1,0:T(8,128)(2,1)S(1)}, u32[]{:S(2)}, u32[]{:S(2)}) collective-permute-start(bf16[128,1664]{1,0:T(8,128)(2,1)S(1)} %get-tuple-element.129), channel_id=1, source_target_pairs={{0,2},{1,3},{2,0},{3,1},{4,6},{5,7},{6,4},{7,5},{8,10},{9,11},{10,... | collective-permute-start | bytes 1277960 | tf_op jit(solution)/shard_map/ppermute | solution.py:75
  716.3 19.9 %collective-permute-start.26 = (bf16[128,1664]{1,0:T(8,128)(2,1)S(1)}, bf16[128,1664]{1,0:T(8,128)(2,1)S(1)}, u32[]{:S(2)}, u32[]{:S(2)}) collective-permute-start(bf16[128,1664]{1,0:T(8,128)(2,1)S(1)} %get-tuple-element.130), channel_id=1, source_target_pairs={{0,2},{1,3},{2,0},{3,1},{4,6},{5,7},{6,4},{7,5},{8,10},{9,11},{10,... | collective-permute-start | bytes 1277960 | tf_op jit(solution)/shard_map/ppermute | solution.py:75
  732.6 11.4 %collective-permute-start.24 = (bf16[128,1536]{1,0:T(8,128)(2,1)S(1)}, bf16[128,1536]{1,0:T(8,128)(2,1)S(1)}, u32[]{:S(2)}, u32[]{:S(2)}) collective-permute-start(bf16[128,1536]{1,0:T(8,128)(2,1)S(1)} %fusion.212), channel_id=1, source_target_pairs={{0,2},{1,3},{2,0},{3,1},{4,6},{5,7},{6,4},{7,5},{8,10},{9,11},{10,... | collective-permute-start | bytes 1179656 | tf_op jit(solution)/shard_map/ppermute | solution.py:75
  736.3 10.2 %collective-permute-start.27 = (bf16[128,1664]{1,0:T(8,128)(2,1)S(1)}, bf16[128,1664]{1,0:T(8,128)(2,1)S(1)}, u32[]{:S(2)}, u32[]{:S(2)}) collective-permute-start(bf16[128,1664]{1,0:T(8,128)(2,1)S(1)} %fusion.208), channel_id=1, source_target_pairs={{0,1},{1,0},{2,3},{3,2},{4,5},{5,4},{6,7},{7,6},{8,9},{9,8},{10,11... | collective-permute-start | bytes 1277960 | tf_op jit(solution)/shard_map/ppermute | solution.py:75
  746.9 9.9 %collective-permute-start.28 = (bf16[32,3200]{1,0:T(8,128)(2,1)S(1)}, bf16[32,3200]{1,0:T(8,128)(2,1)S(1)}, u32[]{:S(2)}, u32[]{:S(2)}) collective-permute-start(bf16[32,3200]{1,0:T(8,128)(2,1)S(1)} %get-tuple-element.141), channel_id=1, source_target_pairs={{0,8},{4,12},{8,16},{12,20},{16,24},{20,28},{24,0},{28,4},{1,9},{5... | collective-permute-start | bytes 614408 | tf_op jit(solution)/shard_map/ppermute | solution.py:70
  746.9 9.9 %collective-permute-start.30 = (bf16[32,3200]{1,0:T(8,128)(2,1)S(1)}, bf16[32,3200]{1,0:T(8,128)(2,1)S(1)}, u32[]{:S(2)}, u32[]{:S(2)}) collective-permute-start(bf16[32,3200]{1,0:T(8,128)(2,1)S(1)} %get-tuple-element.142), channel_id=1, source_target_pairs={{0,24},{4,28},{8,0},{12,4},{16,8},{20,12},{24,16},{28,20},{1,25},{... | collective-permute-start | bytes 614408 | tf_op jit(solution)/shard_map/ppermute | solution.py:70
  750.8 14.3 %collective-permute-start.29 = (bf16[32,3200]{1,0:T(8,128)(2,1)S(1)}, bf16[32,3200]{1,0:T(8,128)(2,1)S(1)}, u32[]{:S(2)}, u32[]{:S(2)}) collective-permute-start(bf16[32,3200]{1,0:T(8,128)(2,1)S(1)} %get-tuple-element.143), channel_id=1, source_target_pairs={{0,16},{4,20},{8,24},{12,28},{16,0},{20,4},{24,8},{28,12},{1,17},{... | collective-permute-start | bytes 614408 | tf_op jit(solution)/shard_map/ppermute | solution.py:70
  765.2 8.1 %collective-permute-start.33 = (bf16[32,3200]{1,0:T(8,128)(2,1)S(1)}, bf16[32,3200]{1,0:T(8,128)(2,1)S(1)}, u32[]{:S(2)}, u32[]{:S(2)}) collective-permute-start(bf16[32,3200]{1,0:T(8,128)(2,1)S(1)} %fusion.233), channel_id=1, source_target_pairs={{0,24},{4,28},{8,0},{12,4},{16,8},{20,12},{24,16},{28,20},{1,25},{... | collective-permute-start | bytes 614408 | tf_op jit(solution)/shard_map/ppermute | solution.py:70
  766.5 15.7 %collective-permute-start.32 = (bf16[32,3200]{1,0:T(8,128)(2,1)S(1)}, bf16[32,3200]{1,0:T(8,128)(2,1)S(1)}, u32[]{:S(2)}, u32[]{:S(2)}) collective-permute-start(bf16[32,3200]{1,0:T(8,128)(2,1)S(1)} %fusion.233), channel_id=1, source_target_pairs={{0,16},{4,20},{8,24},{12,28},{16,0},{20,4},{24,8},{28,12},{1,17},{... | collective-permute-start | bytes 614408 | tf_op jit(solution)/shard_map/ppermute | solution.py:70
  766.5 15.7 %collective-permute-start.31 = (bf16[32,3200]{1,0:T(8,128)(2,1)S(1)}, bf16[32,3200]{1,0:T(8,128)(2,1)S(1)}, u32[]{:S(2)}, u32[]{:S(2)}) collective-permute-start(bf16[32,3200]{1,0:T(8,128)(2,1)S(1)} %fusion.233), channel_id=1, source_target_pairs={{0,8},{4,12},{8,16},{12,20},{16,24},{20,28},{24,0},{28,4},{1,9},{5... | collective-permute-start | bytes 614408 | tf_op jit(solution)/shard_map/ppermute | solution.py:70
  786.0 17.2 %collective-permute-start.34 = (bf16[128,3200]{1,0:T(8,128)(2,1)}, bf16[128,3200]{1,0:T(8,128)(2,1)}, u32[]{:S(2)}, u32[]{:S(2)}) collective-permute-start(bf16[128,3200]{1,0:T(8,128)(2,1)} %bitcast.678), channel_id=1, source_target_pairs={{0,4},{4,0},{8,12},{12,8},{16,20},{20,16},{24,28},{28,24},{1,5},{5... | collective-permute-start | bytes 2457608 | tf_op jit(solution)/shard_map/ppermute | solution.py:67
  (110 other events, 933.5 us)
